TPU v7x, 32 devices: a whole 2x2x4 slice. The times are simulated.
32 devices in a mesh: clusters: 32 (over z, y, x, core).
Axes of the slice: x: 2, y: 2, z: 4, core: 2. Of those that a mesh axis runs over, the one named last changes fastest.
Arguments:
- charges: bfloat16 [8, 131072], P(None, 'clusters'), may hold values from -6 to 6
- leaf_basis: bfloat16 [32, 131072], P(None, 'clusters'), may hold values from -0.75 to 0.75
- leaf_transfer: bfloat16 [256, 64, 256], P('clusters'), may hold values from -0.375 to 0.375
- mid_transfer: bfloat16 [32, 64, 512], P('clusters'), may hold values from -0.25 to 0.25
- far_source: int32 [2048, 16], P('clusters'), may hold values from 0 to 2047, as said below
- far_coupling: bfloat16 [2048, 32, 512], P('clusters'), may hold values from -0.25 to 0.25
- mid_source: int32 [256, 8], P('clusters'), may hold values from 0 to 255, as said below
- mid_coupling: bfloat16 [256, 64, 512], P('clusters'), may hold values from -0.25 to 0.25
- box_coupling: bfloat16 [32, 64, 192], P('clusters'), may hold values from -0.4375 to 0.4375
- top_transfer: bfloat16 [28, 64, 128], replicated, may hold values from -0.5 to 0.5
- top_coupling: bfloat16 [28, 64, 192], replicated, may hold values from -0.4375 to 0.4375
- near_target: int32 [32768], P('clusters'), may hold values from 0 to 63
- near_source: int32 [32768], P('clusters'), may hold values from 0 to 2047, as said below
- near_count: int32 [32], P('clusters'), may hold values from 256 to 1024, as said below
- near_blocks: bfloat16 [64, 2097152], P(None, 'clusters'), may hold values from -0.25 to 0.25
Outputs:
- potentials: bfloat16 [8, 131072], P(None, 'clusters')
Inputs may be any that keep to these rules, and one draw needn't show every extreme that they name: `far_source`: each source leaf lies in the row's box or in a box whose index differs by one; for each box and each box beside it, the far lists of the box's leaves name exactly 4 distinct leaves of the box beside it. `mid_source`: each source cluster lies in the row's box or in a box whose index differs by one. `near_source`: each source leaf lies in the slot's box or in a box whose index differs by one. `near_count`: slots at or after a box's count are not used.
All inputs are finite; a program needn't handle non-finite values.
Results may differ from a plain program's by a relative error of at most 0.0053.
Values may be sent and summed in bfloat16 or wider, within the bound.
A program may use at most 128 MiB of HBM per device.

v0:
```python
import jax
import jax.numpy as jnp
from jax import lax
from jax.sharding import PartitionSpec as P

deepest_level = lax.Precision.HIGHEST


def from_behind(value, axis, steps):
    count = lax.axis_size(axis)
    initial, last = (max(0, -steps), min(count, count - steps))
    return lax.ppermute(value, axis, [(source, source + steps) for source in range(initial, last)])


def partner(block, axis, bit):
    count = lax.axis_size(axis)
    route = []
    for low in range(count):
        high = low | 1 << bit
        if high != low and high < count:
            route += [(low, high), (high, low)]
    return lax.ppermute(block, axis, route)


def with_halo(cells, sides, width):
    for axis, dim in sides:
        count = lax.axis_size(axis)
        ends = count - 1
        head = lax.slice_in_dim(cells, 0, width, axis=dim)
        tail = lax.slice_in_dim(cells, cells.shape[dim] - width, cells.shape[dim], axis=dim)
        cells = jnp.concatenate(
            [
                lax.ppermute(tail, axis, [(i, (i + 1) % count) for i in range(ends)]),
                cells,
                lax.ppermute(head, axis, [((i + 1) % count, i) for i in range(ends)]),
            ],
            axis=dim,
        )
    return cells


def coupling_terms(matrix_stack, stacked):
    return jnp.dot(
        matrix_stack.astype(jnp.float32),
        stacked,
        precision=deepest_level,
        preferred_element_type=jnp.float32,
    )


def arrange_partners(is_even, back_three, back_two, ahead_two, ahead_three):
    return jnp.concatenate(
        [
            jnp.where(is_even, back_two, back_three),
            jnp.where(is_even, ahead_two, back_two),
            jnp.where(is_even, ahead_three, ahead_two),
        ],
        axis=0,
    )


def descend(across_terms, top_transfer, device, devices, levels):
    downward = across_terms[levels]
    rank = downward.shape[0]
    vectors = downward.shape[1]
    for level in range(levels - 1, -1, -1):
        cluster = device >> level
        start = devices - (devices >> level)
        parent_matrix = lax.dynamic_index_in_dim(
            top_transfer, start + (cluster >> 1), 0, keepdims=False
        ).astype(jnp.float32)
        pushed = jnp.dot(
            parent_matrix.T, downward, precision=deepest_level, preferred_element_type=jnp.float32
        ).reshape(2, rank, vectors)
        downward = across_terms[level] + lax.dynamic_index_in_dim(
            pushed, cluster % 2, 0, keepdims=False
        )
    return downward


def level_matrix(box_coupling, top_coupling, level, cluster, devices):
    if level == 0:
        return box_coupling
    start = devices - (devices >> level - 1)
    return lax.dynamic_index_in_dim(top_coupling, start + cluster, 0, keepdims=False)


def top_chain(box_up, box_coupling, top_transfer, top_coupling, device, devices):
    rank = box_up.shape[0]
    vectors = box_up.shape[1]
    levels = (devices // 4).bit_length() - 1
    upward = box_up
    across_terms = []
    for level in range(levels + 1):
        cluster = device >> level
        flat = upward.reshape(1, rank * vectors)
        received = []
        for offset in (-3, -2, 2, 3):
            moved = from_behind(flat, "clusters", -offset * (1 << level))
            received.append(moved.reshape(rank, vectors))
        stacked = arrange_partners(
            cluster % 2 == 0, received[0], received[1], received[2], received[3]
        )
        matrix_stack = level_matrix(box_coupling, top_coupling, level, cluster, devices)
        across_terms.append(coupling_terms(matrix_stack, stacked))
        if level < levels:
            sibling = partner(flat, "clusters", level).reshape(rank, vectors)
            is_left = cluster % 2 == 0
            paired = jnp.concatenate(
                [jnp.where(is_left, upward, sibling), jnp.where(is_left, sibling, upward)], axis=0
            )
            start = devices - (devices >> level)
            parent_matrix = lax.dynamic_index_in_dim(
                top_transfer, start + (cluster >> 1), 0, keepdims=False
            )
            upward = coupling_terms(parent_matrix, paired)
    return descend(across_terms, top_transfer, device, devices, levels)


def near_sum(blocks, fetch, targets, live, turns, block, leaf_count, leaf_capacity, vectors):

    def near_step(step, total):
        first = step * block
        target_rows = lax.dynamic_slice_in_dim(targets, first, block)
        alive = first + jnp.arange(block, dtype=jnp.int32) < live
        dense = lax.dynamic_slice_in_dim(
            blocks, first * leaf_capacity, block * leaf_capacity, 1
        ).reshape(leaf_capacity, block, leaf_capacity)
        gathered = fetch(first)
        contribution = jnp.einsum(
            "tbs,vbs->vbt", dense, gathered, preferred_element_type=jnp.float32
        )
        assignment = (
            (target_rows[:, None] == jnp.arange(leaf_count, dtype=jnp.int32)[None, :])
            & alive[:, None]
        ).astype(jnp.float32)
        return total + jnp.einsum(
            "dn,rdz->rnz",
            assignment,
            contribution,
            precision=deepest_level,
            preferred_element_type=jnp.float32,
        )

    return lax.fori_loop(
        0, turns, near_step, jnp.zeros((vectors, leaf_count, leaf_capacity), jnp.float32)
    )


def body(
    charges,
    leaf_basis,
    leaf_transfer,
    mid_transfer,
    far_source,
    far_coupling,
    mid_source,
    mid_coupling,
    box_coupling,
    top_transfer,
    top_coupling,
    near_target,
    near_source,
    near_count,
    near_blocks,
):
    vectors = charges.shape[0]
    points = charges.shape[1]
    leaf_count = far_source.shape[0]
    leaf_capacity = points // leaf_count
    rank_leaf = leaf_basis.shape[0]
    groups = leaf_transfer.shape[0]
    rank_mid = leaf_transfer.shape[1]
    children = leaf_count // groups
    devices = lax.axis_size("clusters")
    device = lax.axis_index("clusters")
    charge_cube = charges.reshape(vectors, leaf_count, leaf_capacity)
    basis_tensor = leaf_basis.reshape(rank_leaf, leaf_count, leaf_capacity)
    leaf_up = jnp.einsum(
        "rlm,vlm->lrv", basis_tensor, charge_cube, preferred_element_type=jnp.float32
    ).astype(jnp.bfloat16)
    mid_up = jnp.einsum(
        "crk,ckv->crv",
        leaf_transfer,
        leaf_up.reshape(groups, children * rank_leaf, vectors),
        preferred_element_type=jnp.float32,
    ).astype(jnp.bfloat16)
    box_up = jnp.dot(
        mid_transfer[0],
        mid_up.reshape(groups * rank_mid, vectors),
        preferred_element_type=jnp.float32,
    )
    mid_rows = mid_up.reshape(groups, rank_mid * vectors)
    mid_wide = with_halo(mid_rows, (("clusters", 0),), groups)
    leaf_rows = leaf_up.reshape(leaf_count, rank_leaf * vectors)
    sources = far_source.reshape(-1)
    offset = sources - (device - 1) * leaf_count
    leaf_wide = with_halo(leaf_rows, (("clusters", 0),), leaf_count)
    picked = jnp.take(leaf_wide, offset, axis=0)
    leaf_far = jnp.einsum(
        "lrk,lkv->lrv",
        far_coupling,
        picked.reshape(leaf_count, -1, vectors),
        preferred_element_type=jnp.float32,
    )
    mid_index = mid_source.reshape(-1) - (device - 1) * groups
    mid_picked = jnp.take(mid_wide, mid_index, axis=0)
    mid_far = jnp.einsum(
        "crk,ckv->crv",
        mid_coupling,
        mid_picked.reshape(groups, -1, vectors),
        preferred_element_type=jnp.float32,
    )
    box_down = top_chain(box_up, box_coupling[0], top_transfer, top_coupling, device, devices)
    box_low = box_down.astype(jnp.bfloat16)
    mid_push = jnp.einsum(
        "rk,rv->kv", mid_transfer[0], box_low, preferred_element_type=jnp.float32
    ).reshape(groups, rank_mid, vectors)
    mid_down = (mid_far + mid_push).astype(jnp.bfloat16)
    leaf_push = jnp.einsum(
        "crk,crv->ckv", leaf_transfer, mid_down, preferred_element_type=jnp.float32
    ).reshape(leaf_count, rank_leaf, vectors)
    leaf_down = (leaf_far + leaf_push).astype(jnp.bfloat16)
    far_field = jnp.einsum(
        "rlm,lrv->vlm", basis_tensor, leaf_down, preferred_element_type=jnp.float32
    )
    wide = with_halo(charges, (("clusters", 1),), points)
    wide_cube = wide.reshape(vectors, 3 * leaf_count, leaf_capacity)
    capacity = near_target.shape[0]
    quarter = capacity // 4
    block = min(128, quarter)
    local_source = near_source - (device - 1) * leaf_count
    live_count = near_count[0]

    def fetch_local(first):
        return jnp.take(wide_cube, lax.dynamic_slice_in_dim(local_source, first, block), axis=1)

    near_field = near_sum(
        near_blocks,
        fetch_local,
        near_target,
        live_count,
        capacity // block,
        block,
        leaf_count,
        leaf_capacity,
        vectors,
    )
    return (far_field + near_field).astype(jnp.bfloat16).reshape(vectors, points)


def solution(mesh):
    in_specs = (
        P(None, "clusters"),
        P(None, "clusters"),
        P("clusters", None, None),
        P("clusters", None, None),
        P("clusters", None),
        P("clusters", None, None),
        P("clusters", None),
        P("clusters", None, None),
        P("clusters", None, None),
        P(),
        P(),
        P("clusters"),
        P("clusters"),
        P("clusters"),
        P(None, "clusters"),
    )
    out_specs = P(None, "clusters")
    return jax.shard_map(body, mesh=mesh, in_specs=in_specs, out_specs=out_specs, check_vma=False)
```

profile of v0, /device:TPU:1, one launch (start us, length us, event | category | flops | bytes accessed | tf_op | source)
XLA Modules:
  0.0 233.2 jit_solution(12583653071177529908)
XLA Ops:
  0.0 4.6 %collective-permute-start.23 = (bf16[8,4096]{1,0:T(8,128)(2,1)}, bf16[8,4096]{1,0:T(8,128)(2,1)}, u32[]{:S(2)}, u32[]{:S(2)}) collective-permute-start(bf16[8,4096]{1,0:T(8,128)(2,1)} %param.17), channel_id=1, source_target_pairs={{0,1},{1,2},{2,3},{3,4},{4,5},{5,6},{6,7},{7,8},{8,9},{9,10},{10,1... | collective-permute-start | bytes 196616 | tf_op jit(solution)/shard_map/ppermute | solution.py:33
  14.0 5.6 %collective-permute-start.5 = (f32[1,512]{1,0:T(1,128)S(1)}, f32[1,512]{1,0:T(1,128)S(1)}, u32[]{:S(2)}, u32[]{:S(2)}) collective-permute-start(f32[1,512]{1,0:T(1,128)S(1)} %reshape.188), channel_id=1, source_target_pairs={{0,3},{1,4},{2,5},{3,6},{4,7},{5,8},{6,9},{7,10},{8,11},{9,12},{10... | collective-permute-start | bytes 6152 | tf_op jit(solution)/shard_map/ppermute | solution.py:12
  30.6 3.1 %collective-permute-start.13 = (f32[1,512]{1,0:T(1,128)S(1)}, f32[1,512]{1,0:T(1,128)S(1)}, u32[]{:S(2)}, u32[]{:S(2)}) collective-permute-start(f32[1,512]{1,0:T(1,128)S(1)} %reshape.190), channel_id=1, source_target_pairs={{0,2},{2,0},{1,3},{3,1},{4,6},{6,4},{5,7},{7,5},{8,10},{10,8},{9,1... | collective-permute-start | bytes 6152 | tf_op jit(solution)/shard_map/ppermute | solution.py:22
  36.3 5.5 %collective-permute-start.10 = (f32[1,512]{1,0:T(1,128)S(1)}, f32[1,512]{1,0:T(1,128)S(1)}, u32[]{:S(2)}, u32[]{:S(2)}) collective-permute-start(f32[1,512]{1,0:T(1,128)S(1)} %reshape.190), channel_id=1, source_target_pairs={{0,6},{1,7},{2,8},{3,9},{4,10},{5,11},{6,12},{7,13},{8,14},{9,15},... | collective-permute-start | bytes 6152 | tf_op jit(solution)/shard_map/ppermute | solution.py:12
  42.3 4.3 %collective-permute-start.9 = (f32[1,512]{1,0:T(1,128)S(1)}, f32[1,512]{1,0:T(1,128)S(1)}, u32[]{:S(2)}, u32[]{:S(2)}) collective-permute-start(f32[1,512]{1,0:T(1,128)S(1)} %reshape.190), channel_id=1, source_target_pairs={{0,4},{1,5},{2,6},{3,7},{4,8},{5,9},{6,10},{7,11},{8,12},{9,13},{1... | collective-permute-start | bytes 6152 | tf_op jit(solution)/shard_map/ppermute | solution.py:12
  52.4 5.5 %collective-permute-start.15 = (f32[1,512]{1,0:T(1,128)S(1)}, f32[1,512]{1,0:T(1,128)S(1)}, u32[]{:S(2)}, u32[]{:S(2)}) collective-permute-start(f32[1,512]{1,0:T(1,128)S(1)} %reshape.192), channel_id=1, source_target_pairs={{0,12},{1,13},{2,14},{3,15},{4,16},{5,17},{6,18},{7,19},{8,20},{9,... | collective-permute-start | bytes 6152 | tf_op jit(solution)/shard_map/ppermute | solution.py:12
  58.5 3.4 %collective-permute-start.14 = (f32[1,512]{1,0:T(1,128)S(1)}, f32[1,512]{1,0:T(1,128)S(1)}, u32[]{:S(2)}, u32[]{:S(2)}) collective-permute-start(f32[1,512]{1,0:T(1,128)S(1)} %reshape.192), channel_id=1, source_target_pairs={{0,8},{1,9},{2,10},{3,11},{4,12},{5,13},{6,14},{7,15},{8,16},{9,17... | collective-permute-start | bytes 6152 | tf_op jit(solution)/shard_map/ppermute | solution.py:12
  66.3 5.8 %collective-permute-start.20 = (f32[1,512]{1,0:T(1,128)S(1)}, f32[1,512]{1,0:T(1,128)S(1)}, u32[]{:S(2)}, u32[]{:S(2)}) collective-permute-start(f32[1,512]{1,0:T(1,128)S(1)} %reshape.194), channel_id=1, source_target_pairs={{0,24},{1,25},{2,26},{3,27},{4,28},{5,29},{6,30},{7,31}} | collective-permute-start | bytes 6152 | tf_op jit(solution)/shard_map/ppermute | solution.py:12
  73.9 5.8 %collective-permute-start.24 = (bf16[8,4096]{1,0:T(8,128)(2,1)S(1)}, bf16[8,4096]{1,0:T(8,128)(2,1)}, u32[]{:S(2)}, u32[]{:S(2)}) collective-permute-start(bf16[8,4096]{1,0:T(8,128)(2,1)S(1)} %copy-done.4), channel_id=1, source_target_pairs={{1,0},{2,1},{3,2},{4,3},{5,4},{6,5},{7,6},{8,7},{9,8},{10,9},{11,1... | collective-permute-start | bytes 196616 | tf_op jit(solution)/shard_map/ppermute | solution.py:35
  81.6 3.6 %collective-permute-start.2 = (bf16[8,512]{1,0:T(8,128)(2,1)S(1)}, bf16[8,512]{1,0:T(8,128)(2,1)S(1)}, u32[]{:S(2)}, u32[]{:S(2)}) collective-permute-start(bf16[8,512]{1,0:T(8,128)(2,1)S(1)} %reshape.186), channel_id=1, source_target_pairs={{0,1},{1,2},{2,3},{3,4},{4,5},{5,6},{6,7},{7,8},{8,9},{9,10},{10,1... | collective-permute-start | bytes 24584 | tf_op jit(solution)/shard_map/ppermute | solution.py:33
  92.4 3.8 %collective-permute-start = (bf16[64,256]{1,0:T(8,128)(2,1)}, bf16[64,256]{1,0:T(8,128)(2,1)}, u32[]{:S(2)}, u32[]{:S(2)}) collective-permute-start(bf16[64,256]{1,0:T(8,128)(2,1)} %copy.155), channel_id=1, source_target_pairs={{0,1},{1,2},{2,3},{3,4},{4,5},{5,6},{6,7},{7,8},{8,9},{9,10},{10,1... | collective-permute-start | bytes 98312 | tf_op jit(solution)/shard_map/ppermute | solution.py:33
  101.9 3.9 %gather_fusion.1 = bf16[1024,256]{1,0:T(8,128)(2,1)S(1)} fusion(bf16[192,256]{1,0:T(8,128)(2,1)S(1)} %pad_maximum_fusion.1, s32[1024]{0:T(1024)S(1)} %broadcast_clamp_fusion), kind=kCustom, calls=%fused_computation.1 | custom fusion | bytes 1052672 | tf_op jit(solution)/shard_map/jit(_take)/gather | solution.py:199
  105.9 10.8 %gather.24 = bf16[64,512,8]{2,1,0:T(8,128)(2,1)} reshape(bf16[1024,256]{1,0:T(8,128)(2,1)S(1)} %gather_fusion.1) | data formatting | bytes 1048576 | tf_op jit(solution)/shard_map/jit(_take)/gather | solution.py:199
  118.9 102.9 %while.16 = (s32[]{:T(128)}, f32[8,64,64]{1,2,0:T(8,128)}, s32[1024]{0:T(1024)S(1)}, bf16[8,192,64]{2,0,1:T(8,128)(2,1)}, bf16[64,65536]{1,0:T(8,128)(2,1)}, /*i...) while((s32[]{:T(128)}, f32[8,64,64]{1,2,0:T(8,128)}, ...), condition=%wide.region_1.2_spmd.clone, body=%wide.region_0.1_spmd.clone.sunk | while | flops 58869768 | bytes 6430975 | solution.py:145
  123.4 3.3 %reshape.319 = bf16[64,128,64]{2,1,0:T(8,128)(2,1)} reshape(bf16[64,8192]{1,0:T(8,128)(2,1)S(1)} %constant_dynamic-slice_fusion.2) | data formatting | bytes 2097152 | tf_op jit(solution)/shard_map/while/body/eval_jaxpr/reshape | solution.py:128
  135.4 3.3 %reshape.319 = bf16[64,128,64]{2,1,0:T(8,128)(2,1)} reshape(bf16[64,8192]{1,0:T(8,128)(2,1)S(1)} %constant_dynamic-slice_fusion.2) | data formatting | bytes 2097152 | tf_op jit(solution)/shard_map/while/body/eval_jaxpr/reshape | solution.py:128
  148.4 3.3 %reshape.319 = bf16[64,128,64]{2,1,0:T(8,128)(2,1)} reshape(bf16[64,8192]{1,0:T(8,128)(2,1)S(1)} %constant_dynamic-slice_fusion.2) | data formatting | bytes 2097152 | tf_op jit(solution)/shard_map/while/body/eval_jaxpr/reshape | solution.py:128
  151.7 3.0 %fusion.156 = f32[8,128,64]{2,0,1:T(8,128)S(1)} fusion(bf16[64,128,64]{2,1,0:T(8,128)(2,1)} %reshape.319, bf16[128,8,64]{2,1,0:T(8,128)(2,1)S(1)} %gather_fusion, pred[128]{0:T(512)(128)(4,1)S(1)} %get-tuple-element.323), kind=kOutput, calls=%fused_computation.5.clone.1 | convolution fusion | flops 8454144 | bytes 1441920 | tf_op jit(solution)/shard_map/while/body/eval_jaxpr/tbs,vbs->vbt/dot_general | solution.py:130
  161.4 3.3 %reshape.319 = bf16[64,128,64]{2,1,0:T(8,128)(2,1)} reshape(bf16[64,8192]{1,0:T(8,128)(2,1)S(1)} %constant_dynamic-slice_fusion.2) | data formatting | bytes 2097152 | tf_op jit(solution)/shard_map/while/body/eval_jaxpr/reshape | solution.py:128
  174.4 3.3 %reshape.319 = bf16[64,128,64]{2,1,0:T(8,128)(2,1)} reshape(bf16[64,8192]{1,0:T(8,128)(2,1)S(1)} %constant_dynamic-slice_fusion.2) | data formatting | bytes 2097152 | tf_op jit(solution)/shard_map/while/body/eval_jaxpr/reshape | solution.py:128
  187.4 3.3 %reshape.319 = bf16[64,128,64]{2,1,0:T(8,128)(2,1)} reshape(bf16[64,8192]{1,0:T(8,128)(2,1)S(1)} %constant_dynamic-slice_fusion.2) | data formatting | bytes 2097152 | tf_op jit(solution)/shard_map/while/body/eval_jaxpr/reshape | solution.py:128
  200.3 3.3 %reshape.319 = bf16[64,128,64]{2,1,0:T(8,128)(2,1)} reshape(bf16[64,8192]{1,0:T(8,128)(2,1)S(1)} %constant_dynamic-slice_fusion.2) | data formatting | bytes 2097152 | tf_op jit(solution)/shard_map/while/body/eval_jaxpr/reshape | solution.py:128
  213.3 3.3 %reshape.319 = bf16[64,128,64]{2,1,0:T(8,128)(2,1)} reshape(bf16[64,8192]{1,0:T(8,128)(2,1)S(1)} %constant_dynamic-slice_fusion.2) | data formatting | bytes 2097152 | tf_op jit(solution)/shard_map/while/body/eval_jaxpr/reshape | solution.py:128
  222.9 9.5 %fusion.31 = bf16[8,64,64]{2,0,1:T(8,128)(2,1)S(1)} fusion(f32[8,64,64]{2,0,1:T(8,128)S(1)} %copy.195, bf16[64,32,512]{2,1,0:T(8,128)(2,1)S(1)} %copy-done, bf16[64,512,8]{2,1,0:T(8,128)(2,1)} %gather.24, pred[64,512]{1,0:T(8,128)(4,1)S(1)} %copy-done.5, bf16[32,64,64]{2,1,0:T(8,128)(2,1)} %copy-done.1, f32[64,32,8]{1,0,2:T(8,128)} %reshape.196), kind=kOutput, calls=%fused_computation.33 | convolution fusion | flops 19234816 | bytes 3178496 | tf_op jit(solution)/shard_map/rlm,lrv->vlm/dot_general | solution.py:224
  (213 shorter events, 128.2 us)
Async XLA Ops:
  0.0 116.6 %collective-permute-start.23 = (bf16[8,4096]{1,0:T(8,128)(2,1)}, bf16[8,4096]{1,0:T(8,128)(2,1)}, u32[]{:S(2)}, u32[]{:S(2)}) collective-permute-start(bf16[8,4096]{1,0:T(8,128)(2,1)} %param.17), channel_id=1, source_target_pairs={{0,1},{1,2},{2,3},{3,4},{4,5},{5,6},{6,7},{7,8},{8,9},{9,10},{10,1... | collective-permute-start | bytes 196616 | tf_op jit(solution)/shard_map/ppermute | solution.py:33
  11.3 13.8 %collective-permute-start.8 = (f32[1,512]{1,0:T(1,128)S(1)}, f32[1,512]{1,0:T(1,128)S(1)}, u32[]{:S(2)}, u32[]{:S(2)}) collective-permute-start(f32[1,512]{1,0:T(1,128)S(1)} %reshape.188), channel_id=1, source_target_pairs={{0,1},{1,0},{2,3},{3,2},{4,5},{5,4},{6,7},{7,6},{8,9},{9,8},{10,11... | collective-permute-start | bytes 6152 | tf_op jit(solution)/shard_map/ppermute | solution.py:22
  11.4 19.2 %collective-permute-start.7 = (f32[1,512]{1,0:T(1,128)S(1)}, f32[1,512]{1,0:T(1,128)S(1)}, u32[]{:S(2)}, u32[]{:S(2)}) collective-permute-start(f32[1,512]{1,0:T(1,128)S(1)} %reshape.188), channel_id=1, source_target_pairs={{3,0},{4,1},{5,2},{6,3},{7,4},{8,5},{9,6},{10,7},{11,8},{12,9},{13... | collective-permute-start | bytes 6152 | tf_op jit(solution)/shard_map/ppermute | solution.py:12
  12.7 21.0 %collective-permute-start.6 = (f32[1,512]{1,0:T(1,128)S(1)}, f32[1,512]{1,0:T(1,128)S(1)}, u32[]{:S(2)}, u32[]{:S(2)}) collective-permute-start(f32[1,512]{1,0:T(1,128)S(1)} %reshape.188), channel_id=1, source_target_pairs={{2,0},{3,1},{4,2},{5,3},{6,4},{7,5},{8,6},{9,7},{10,8},{11,9},{12,... | collective-permute-start | bytes 6152 | tf_op jit(solution)/shard_map/ppermute | solution.py:12
  14.0 20.9 %collective-permute-start.5 = (f32[1,512]{1,0:T(1,128)S(1)}, f32[1,512]{1,0:T(1,128)S(1)}, u32[]{:S(2)}, u32[]{:S(2)}) collective-permute-start(f32[1,512]{1,0:T(1,128)S(1)} %reshape.188), channel_id=1, source_target_pairs={{0,3},{1,4},{2,5},{3,6},{4,7},{5,8},{6,9},{7,10},{8,11},{9,12},{10... | collective-permute-start | bytes 6152 | tf_op jit(solution)/shard_map/ppermute | solution.py:12
  25.1 11.1 %collective-permute-start.4 = (f32[1,512]{1,0:T(1,128)S(1)}, f32[1,512]{1,0:T(1,128)S(1)}, u32[]{:S(2)}, u32[]{:S(2)}) collective-permute-start(f32[1,512]{1,0:T(1,128)S(1)} %reshape.188), channel_id=1, source_target_pairs={{0,2},{1,3},{2,4},{3,5},{4,6},{5,7},{6,8},{7,9},{8,10},{9,11},{10,... | collective-permute-start | bytes 6152 | tf_op jit(solution)/shard_map/ppermute | solution.py:12
  30.6 11.7 %collective-permute-start.13 = (f32[1,512]{1,0:T(1,128)S(1)}, f32[1,512]{1,0:T(1,128)S(1)}, u32[]{:S(2)}, u32[]{:S(2)}) collective-permute-start(f32[1,512]{1,0:T(1,128)S(1)} %reshape.190), channel_id=1, source_target_pairs={{0,2},{2,0},{1,3},{3,1},{4,6},{6,4},{5,7},{7,5},{8,10},{10,8},{9,1... | collective-permute-start | bytes 6152 | tf_op jit(solution)/shard_map/ppermute | solution.py:22
  33.7 14.8 %collective-permute-start.12 = (f32[1,512]{1,0:T(1,128)S(1)}, f32[1,512]{1,0:T(1,128)S(1)}, u32[]{:S(2)}, u32[]{:S(2)}) collective-permute-start(f32[1,512]{1,0:T(1,128)S(1)} %reshape.190), channel_id=1, source_target_pairs={{6,0},{7,1},{8,2},{9,3},{10,4},{11,5},{12,6},{13,7},{14,8},{15,9},... | collective-permute-start | bytes 6152 | tf_op jit(solution)/shard_map/ppermute | solution.py:12
  35.0 14.9 %collective-permute-start.11 = (f32[1,512]{1,0:T(1,128)S(1)}, f32[1,512]{1,0:T(1,128)S(1)}, u32[]{:S(2)}, u32[]{:S(2)}) collective-permute-start(f32[1,512]{1,0:T(1,128)S(1)} %reshape.190), channel_id=1, source_target_pairs={{4,0},{5,1},{6,2},{7,3},{8,4},{9,5},{10,6},{11,7},{12,8},{13,9},{1... | collective-permute-start | bytes 6152 | tf_op jit(solution)/shard_map/ppermute | solution.py:12
  36.3 14.8 %collective-permute-start.10 = (f32[1,512]{1,0:T(1,128)S(1)}, f32[1,512]{1,0:T(1,128)S(1)}, u32[]{:S(2)}, u32[]{:S(2)}) collective-permute-start(f32[1,512]{1,0:T(1,128)S(1)} %reshape.190), channel_id=1, source_target_pairs={{0,6},{1,7},{2,8},{3,9},{4,10},{5,11},{6,12},{7,13},{8,14},{9,15},... | collective-permute-start | bytes 6152 | tf_op jit(solution)/shard_map/ppermute | solution.py:12
  42.3 10.1 %collective-permute-start.9 = (f32[1,512]{1,0:T(1,128)S(1)}, f32[1,512]{1,0:T(1,128)S(1)}, u32[]{:S(2)}, u32[]{:S(2)}) collective-permute-start(f32[1,512]{1,0:T(1,128)S(1)} %reshape.190), channel_id=1, source_target_pairs={{0,4},{1,5},{2,6},{3,7},{4,8},{5,9},{6,10},{7,11},{8,12},{9,13},{1... | collective-permute-start | bytes 6152 | tf_op jit(solution)/shard_map/ppermute | solution.py:12
  48.5 10.0 %collective-permute-start.18 = (f32[1,512]{1,0:T(1,128)S(1)}, f32[1,512]{1,0:T(1,128)S(1)}, u32[]{:S(2)}, u32[]{:S(2)}) collective-permute-start(f32[1,512]{1,0:T(1,128)S(1)} %reshape.192), channel_id=1, source_target_pairs={{0,4},{4,0},{1,5},{5,1},{2,6},{6,2},{3,7},{7,3},{8,12},{12,8},{9,1... | collective-permute-start | bytes 6152 | tf_op jit(solution)/shard_map/ppermute | solution.py:22
  49.8 13.9 %collective-permute-start.17 = (f32[1,512]{1,0:T(1,128)S(1)}, f32[1,512]{1,0:T(1,128)S(1)}, u32[]{:S(2)}, u32[]{:S(2)}) collective-permute-start(f32[1,512]{1,0:T(1,128)S(1)} %reshape.192), channel_id=1, source_target_pairs={{12,0},{13,1},{14,2},{15,3},{16,4},{17,5},{18,6},{19,7},{20,8},{21... | collective-permute-start | bytes 6152 | tf_op jit(solution)/shard_map/ppermute | solution.py:12
  51.1 13.9 %collective-permute-start.16 = (f32[1,512]{1,0:T(1,128)S(1)}, f32[1,512]{1,0:T(1,128)S(1)}, u32[]{:S(2)}, u32[]{:S(2)}) collective-permute-start(f32[1,512]{1,0:T(1,128)S(1)} %reshape.192), channel_id=1, source_target_pairs={{8,0},{9,1},{10,2},{11,3},{12,4},{13,5},{14,6},{15,7},{16,8},{17,9... | collective-permute-start | bytes 6152 | tf_op jit(solution)/shard_map/ppermute | solution.py:12
  52.4 13.9 %collective-permute-start.15 = (f32[1,512]{1,0:T(1,128)S(1)}, f32[1,512]{1,0:T(1,128)S(1)}, u32[]{:S(2)}, u32[]{:S(2)}) collective-permute-start(f32[1,512]{1,0:T(1,128)S(1)} %reshape.192), channel_id=1, source_target_pairs={{0,12},{1,13},{2,14},{3,15},{4,16},{5,17},{6,18},{7,19},{8,20},{9,... | collective-permute-start | bytes 6152 | tf_op jit(solution)/shard_map/ppermute | solution.py:12
  58.5 13.6 %collective-permute-start.14 = (f32[1,512]{1,0:T(1,128)S(1)}, f32[1,512]{1,0:T(1,128)S(1)}, u32[]{:S(2)}, u32[]{:S(2)}) collective-permute-start(f32[1,512]{1,0:T(1,128)S(1)} %reshape.192), channel_id=1, source_target_pairs={{0,8},{1,9},{2,10},{3,11},{4,12},{5,13},{6,14},{7,15},{8,16},{9,17... | collective-permute-start | bytes 6152 | tf_op jit(solution)/shard_map/ppermute | solution.py:12
  63.7 10.2 %collective-permute-start.22 = (f32[1,512]{1,0:T(1,128)S(1)}, f32[1,512]{1,0:T(1,128)S(1)}, u32[]{:S(2)}, u32[]{:S(2)}) collective-permute-start(f32[1,512]{1,0:T(1,128)S(1)} %reshape.194), channel_id=1, source_target_pairs={{24,0},{25,1},{26,2},{27,3},{28,4},{29,5},{30,6},{31,7}} | collective-permute-start | bytes 6152 | tf_op jit(solution)/shard_map/ppermute | solution.py:12
  65.0 14.7 %collective-permute-start.21 = (f32[1,512]{1,0:T(1,128)S(1)}, f32[1,512]{1,0:T(1,128)S(1)}, u32[]{:S(2)}, u32[]{:S(2)}) collective-permute-start(f32[1,512]{1,0:T(1,128)S(1)} %reshape.194), channel_id=1, source_target_pairs={{16,0},{17,1},{18,2},{19,3},{20,4},{21,5},{22,6},{23,7},{24,8},{25... | collective-permute-start | bytes 6152 | tf_op jit(solution)/shard_map/ppermute | solution.py:12
  66.3 15.3 %collective-permute-start.20 = (f32[1,512]{1,0:T(1,128)S(1)}, f32[1,512]{1,0:T(1,128)S(1)}, u32[]{:S(2)}, u32[]{:S(2)}) collective-permute-start(f32[1,512]{1,0:T(1,128)S(1)} %reshape.194), channel_id=1, source_target_pairs={{0,24},{1,25},{2,26},{3,27},{4,28},{5,29},{6,30},{7,31}} | collective-permute-start | bytes 6152 | tf_op jit(solution)/shard_map/ppermute | solution.py:12
  72.1 13.2 %collective-permute-start.19 = (f32[1,512]{1,0:T(1,128)S(1)}, f32[1,512]{1,0:T(1,128)S(1)}, u32[]{:S(2)}, u32[]{:S(2)}) collective-permute-start(f32[1,512]{1,0:T(1,128)S(1)} %reshape.194), channel_id=1, source_target_pairs={{0,16},{1,17},{2,18},{3,19},{4,20},{5,21},{6,22},{7,23},{8,24},{9,... | collective-permute-start | bytes 6152 | tf_op jit(solution)/shard_map/ppermute | solution.py:12
  73.9 42.7 %collective-permute-start.24 = (bf16[8,4096]{1,0:T(8,128)(2,1)S(1)}, bf16[8,4096]{1,0:T(8,128)(2,1)}, u32[]{:S(2)}, u32[]{:S(2)}) collective-permute-start(bf16[8,4096]{1,0:T(8,128)(2,1)S(1)} %copy-done.4), channel_id=1, source_target_pairs={{1,0},{2,1},{3,2},{4,3},{5,4},{6,5},{7,6},{8,7},{9,8},{10,9},{11,1... | collective-permute-start | bytes 196616 | tf_op jit(solution)/shard_map/ppermute | solution.py:35
  79.7 12.7 %collective-permute-start.3 = (bf16[8,512]{1,0:T(8,128)(2,1)S(1)}, bf16[8,512]{1,0:T(8,128)(2,1)S(1)}, u32[]{:S(2)}, u32[]{:S(2)}) collective-permute-start(bf16[8,512]{1,0:T(8,128)(2,1)S(1)} %reshape.186), channel_id=1, source_target_pairs={{1,0},{2,1},{3,2},{4,3},{5,4},{6,5},{7,6},{8,7},{9,8},{10,9},{11,1... | collective-permute-start | bytes 24584 | tf_op jit(solution)/shard_map/ppermute | solution.py:35
  81.6 14.6 %collective-permute-start.2 = (bf16[8,512]{1,0:T(8,128)(2,1)S(1)}, bf16[8,512]{1,0:T(8,128)(2,1)S(1)}, u32[]{:S(2)}, u32[]{:S(2)}) collective-permute-start(bf16[8,512]{1,0:T(8,128)(2,1)S(1)} %reshape.186), channel_id=1, source_target_pairs={{0,1},{1,2},{2,3},{3,4},{4,5},{5,6},{6,7},{7,8},{8,9},{9,10},{10,1... | collective-permute-start | bytes 24584 | tf_op jit(solution)/shard_map/ppermute | solution.py:33
  85.3 15.8 %collective-permute-start.1 = (bf16[64,256]{1,0:T(8,128)(2,1)}, bf16[64,256]{1,0:T(8,128)(2,1)}, u32[]{:S(2)}, u32[]{:S(2)}) collective-permute-start(bf16[64,256]{1,0:T(8,128)(2,1)} %copy.155), channel_id=1, source_target_pairs={{1,0},{2,1},{3,2},{4,3},{5,4},{6,5},{7,6},{8,7},{9,8},{10,9},{11,1... | collective-permute-start | bytes 98312 | tf_op jit(solution)/shard_map/ppermute | solution.py:35
  (8 other events, 691.2 us)
where the time goes:
time: 237 us; the launch traced here: 233 us
  local copies, waits for them, and re-layouts  88.1 us (37%)
  starting transfers between devices  70.7 us (30%)
  matrix products  61.8 us (26%)
  other arithmetic  11.7 us (5%)
    ppermute x16, starting transfers between devices, from_behind(): lax.ppermute(value, axis, [(source, source + steps) for source in range(i...  44.6 us
    reshape x8, local copies, waits for them, and re-layouts, near_step(): dense = lax.dynamic_slice_in_dim(blocks, first * leaf_capacity, block * l...  26.1 us
    dot_general x8, matrix products, near_step(): jnp.einsum('tbs,vbs->vbt', dense, gathered, preferred_element_type=jnp.fl...  24 us
    dot_general x8, matrix products, near_step(): jnp.einsum('dn,rdz->rnz', assignment, contribution, precision=deepest_lev...  17.1 us
    gather x2, local copies, waits for them, and re-layouts, body(): picked = jnp.take(leaf_wide, offset, axis=0)  14.7 us
    gather x8, local copies, waits for them, and re-layouts, fetch_local(): jnp.take(wide_cube, lax.dynamic_slice_in_dim(local_source, first, block),...  13.4 us
    ppermute x3, starting transfers between devices, with_halo(): lax.ppermute(tail, axis, [(i, (i + 1) % count) for i in range(ends)])  12.1 us
    dynamic_slice x8, local copies, waits for them, and re-layouts, near_step(): lax.dynamic_slice_in_dim(blocks, first * leaf_capacity, block * leaf_capa...  10.4 us
  transfers between devices with their start and end apart: 25, of which 0 were waited for; matrix products, arithmetic and copies ran while one was open for 19% of the time, Pallas kernels for 0%

commit v1 on v0

v1 whole, which is shorter than its diff:
```python
import functools

import jax
import jax.numpy as jnp
from jax import lax
from jax.experimental import pallas as pl
from jax.experimental.pallas import tpu as pltpu
from jax.sharding import PartitionSpec as P

F32 = jnp.float32
BF16 = jnp.bfloat16
AXIS = "clusters"
NT = (((1,), (1,)), ((), ()))
NN = (((1,), (0,)), ((), ()))
LANES = 128
CHUNKS = 8


def dot_nt(a, b):
    return lax.dot_general(a, b, NT, preferred_element_type=F32)


def dot_nn(a, b):
    return lax.dot_general(a, b, NN, preferred_element_type=F32)


def lanes(shape):
    return lax.broadcasted_iota(jnp.int32, shape, len(shape) - 1)


def rows(shape):
    return lax.broadcasted_iota(jnp.int32, shape, len(shape) - 2)


def split(x):
    high = x.astype(BF16).astype(F32)
    return jnp.concatenate([high, x - high], axis=0).astype(BF16)


def exact_nt(x, matrix):
    v = x.shape[0]
    out = dot_nt(split(x), matrix)
    return out[:v] + out[v:]


def exact_nn(x, matrix):
    v = x.shape[0]
    out = dot_nn(split(x), matrix)
    return out[:v] + out[v:]


def diagonal(out, v, width):
    blocks = out.shape[0] // v
    lane = lanes((v, out.shape[1])) // width
    total = jnp.zeros((v, out.shape[1]), F32)
    for block in range(blocks):
        total = jnp.where(lane == block, out[block * v:(block + 1) * v], total)
    return total


def kernel(
    n, sizes,
    near_source, far_source, mid_source, near_count, near_target,
    charges_h, basis_h, leaf_transfer_h, mid_transfer_h, far_coupling_h, mid_coupling_h,
    box_coupling_h, top_transfer_h, top_coupling_h, near_blocks_h,
    out_ref,
    cw, lw, mw, gathered, basis, leaf_transfer, mid_transfer, far_coupling, mid_coupling,
    box_coupling, top_transfer, top_coupling, near_blocks,
    charge_tiles, leaf_tiles, mid_tiles, contribution, near_rows, leaf_far, mid_far, masked_basis, upward,
    load_sem, near_sem, top_sem, halo_send, halo_recv, all_send, all_recv,
):
    v, leaves, m, r0, groups, r, k0, k1, capacity = sizes
    child = leaves // groups
    levels = (n // 4).bit_length() - 1
    me = lax.axis_index(AXIS)
    half = lanes((v, LANES)) < m
    low_lane = lanes((v, LANES)) < r

    barrier = pltpu.get_barrier_semaphore()

    def greet(step, carry):
        other = lax.rem(me + step, n)
        pl.semaphore_signal(barrier, inc=1, device_id=(other,), device_id_type=pl.DeviceIdType.MESH)
        return carry

    lax.fori_loop(1, n, greet, 0)

    pairs = [
        (charges_h, cw.at[1]), (basis_h, basis), (leaf_transfer_h, leaf_transfer), (mid_transfer_h.at[0], mid_transfer),
        (mid_coupling_h, mid_coupling), (far_coupling_h, far_coupling), (box_coupling_h.at[0], box_coupling),
        (top_transfer_h, top_transfer),
    ]
    loads = [pltpu.make_async_copy(s, d, load_sem.at[i]) for i, (s, d) in enumerate(pairs)]
    width = near_blocks.shape[1] // CHUNKS

    def near_load(chunk):
        span = pl.ds(pl.multiple_of(chunk * width, width), width)
        return pltpu.make_async_copy(near_blocks_h.at[:, span], near_blocks.at[:, span], near_sem.at[chunk])

    for i in range(4):
        loads[i].start()
    for chunk in range(CHUNKS):
        near_load(chunk).start()
    for i in range(4, len(loads)):
        loads[i].start()
    tops = []
    for level in range(1, levels + 1):
        start = n - (n >> (level - 1))
        tops.append(pltpu.make_async_copy(
            top_coupling_h.at[start + (me >> level)], top_coupling.at[level - 1], top_sem.at[level - 1]))
    for copy in tops:
        copy.start()

    loads[0].wait()
    loads[1].wait()
    span_points = child * m
    lane_leaf = lanes((v, span_points)) // m
    ups = []
    for c in range(groups):
        x = cw[1, :, c * span_points:(c + 1) * span_points].astype(F32)
        lhs = jnp.concatenate([jnp.where(lane_leaf == l, x, 0.0) for l in range(child)], axis=0).astype(BF16)
        b = basis[:, c * span_points:(c + 1) * span_points]
        up = diagonal(dot_nt(lhs, jnp.concatenate([b] * child, axis=0)), v, r0).astype(BF16)
        lw[1, :, c * child * r0:(c + 1) * child * r0] = up
        ups.append(up.astype(F32))
    loads[2].wait()
    loads[3].wait()
    quad = 4
    for g in range(groups // quad):
        lhs = jnp.concatenate(ups[g * quad:(g + 1) * quad], axis=0).astype(BF16)
        matrix = leaf_transfer[g * quad:(g + 1) * quad].reshape(quad * r, child * r0)
        mw[1, :, g * quad * r:(g + 1) * quad * r] = diagonal(dot_nt(lhs, matrix), v, r).astype(BF16)
    transfer = mid_transfer[...]
    box_up = dot_nt(mw[1], jnp.concatenate([transfer, transfer], axis=0))
    gathered[me] = box_up

    pl.semaphore_wait(barrier, n - 1)

    def everyone(step):
        other = lax.rem(me + step, n)
        return pltpu.make_async_remote_copy(
            src_ref=gathered.at[me], dst_ref=gathered.at[me], send_sem=all_send.at[step],
            recv_sem=all_recv.at[me], device_id=(other,), device_id_type=pl.DeviceIdType.MESH)

    def arrival(source):
        return pltpu.make_async_remote_copy(
            src_ref=gathered.at[source], dst_ref=gathered.at[source], send_sem=all_send.at[0],
            recv_sem=all_recv.at[source], device_id=(me,), device_id_type=pl.DeviceIdType.MESH)

    wides = (cw, lw, mw)

    def halo(kind, side):
        wide = wides[kind]
        return pltpu.make_async_remote_copy(
            src_ref=wide.at[1], dst_ref=wide.at[2 - 2 * side], send_sem=halo_send.at[2 * kind + side],
            recv_sem=halo_recv.at[2 * kind + side], device_id=(me - 1 + 2 * side,),
            device_id_type=pl.DeviceIdType.MESH)

    def halo_starts(kind):
        @pl.when(me > 0)
        def _():
            halo(kind, 0).start()

        @pl.when(me < n - 1)
        def _():
            halo(kind, 1).start()

    def halo_arrive(kind):
        wide = wides[kind]

        @pl.when(me < n - 1)
        def _():
            halo(kind, 0).wait_recv()

        @pl.when(me > 0)
        def _():
            halo(kind, 1).wait_recv()

        @pl.when(me == 0)
        def _():
            wide[0] = jnp.zeros(wide.shape[1:], BF16)

        @pl.when(me == n - 1)
        def _():
            wide[2] = jnp.zeros(wide.shape[1:], BF16)

    def halo_sent(kind):
        @pl.when(me > 0)
        def _():
            halo(kind, 0).wait_send()

        @pl.when(me < n - 1)
        def _():
            halo(kind, 1).wait_send()

    halo_starts(0)

    def send_step(step, carry):
        everyone(step).start()
        return carry

    lax.fori_loop(1, n, send_step, 0)
    halo_starts(1)
    halo_starts(2)

    quad_mask = (rows((4 * r0, 4 * m)) // r0 == lanes((4 * r0, 4 * m)) // m).astype(F32).astype(BF16)
    for q in range(leaves // 4):
        b = basis[:, q * 4 * m:(q + 1) * 4 * m]
        masked_basis[q] = jnp.concatenate([b] * 4, axis=0) * quad_mask
    count = near_count[0]
    leaf_row = rows((leaves, LANES))
    slot_lane = lanes((leaves, LANES))
    assignment = []
    for b in range(capacity // LANES):
        hit = (leaf_row == near_target[b:b + 1, :]) & (slot_lane + b * LANES < count)
        assignment.append(jnp.where(hit, 1.0, 0.0).astype(BF16))

    def spread_pairs(wide, tiles, per_box, box):
        x = wide[box].astype(F32)
        first = lax.rem(me + 3 + box, 4) * per_box
        for t in range(per_box // 2):
            tile = x[:, t * LANES:(t + 1) * LANES]
            turned = pltpu.roll(tile, LANES // 2, 1)
            tiles[first + 2 * t] = jnp.where(half, tile, turned)
            tiles[first + 2 * t + 1] = jnp.where(half, turned, tile)

    fold = LANES // r0
    lane_block = lanes((v, LANES)) // r0

    def spread_leaves(box):
        x = lw[box].astype(F32)
        first = lax.rem(me + 3 + box, 4) * leaves
        for t in range(leaves // fold):
            tile = x[:, t * LANES:(t + 1) * LANES]
            turned = [tile] + [pltpu.roll(tile, r0 * k, 1) for k in range(1, fold)]
            for p in range(fold):
                piece = turned[(0 - p) % fold]
                for w in range(1, fold):
                    piece = jnp.where(lane_block == w, turned[(w - p) % fold], piece)
                leaf_tiles[first + t * fold + p] = piece

    for tiles, per_box in ((charge_tiles, leaves), (leaf_tiles, leaves), (mid_tiles, groups)):
        unused = pl.ds(lax.rem(me + 2, 4) * per_box, per_box)
        tiles[unused] = jnp.zeros((per_box, v, LANES), F32)
    spread_pairs(cw, charge_tiles, leaves, 1)
    halo_arrive(0)
    spread_pairs(cw, charge_tiles, leaves, 0)
    spread_pairs(cw, charge_tiles, leaves, 2)

    block = 32
    zero = jnp.zeros((2 * v, LANES), F32)
    steps_per_chunk = capacity // CHUNKS // block

    def near_step(step, carry):
        base = step * block
        for g in range(block // 4):
            pieces = []
            for i in range(4):
                x = charge_tiles[near_source[base + g * 4 + i] & (4 * leaves - 1)]
                pieces.append(jnp.where(half, x, 0.0) if i % 2 == 0 else jnp.where(half, 0.0, x))
            upper = jnp.concatenate([pieces[0], pieces[1]], axis=0)
            lower = jnp.concatenate([pieces[2], pieces[3]], axis=0)
            lhs = jnp.concatenate(
                [jnp.concatenate([upper, zero], axis=1), jnp.concatenate([zero, lower], axis=1)], axis=0).astype(BF16)
            span = pl.ds(pl.multiple_of(base * m + g * 4 * m, 4 * m), 4 * m)
            contribution[pl.ds(pl.multiple_of((base + g * 4) * v, 4 * v), 4 * v), :] = dot_nt(lhs, near_blocks[:, span])
        return carry

    def near_chunk(chunk, carry):
        near_load(chunk).wait()
        return lax.fori_loop(chunk * steps_per_chunk, (chunk + 1) * steps_per_chunk, near_step, carry)

    lax.fori_loop(0, CHUNKS, near_chunk, 0)

    for u in range(v):
        total = jnp.zeros((leaves, 2 * m), F32)
        for b in range(capacity // LANES):
            c = contribution[pl.ds(b * LANES * v + u, LANES, stride=v), :]
            high = c.astype(BF16)
            low = (c - high.astype(F32)).astype(BF16)
            total = total + dot_nn(assignment[b], jnp.concatenate([high, low], axis=1))
        near_rows[u * leaves:(u + 1) * leaves, :] = total

    halo_arrive(1)
    for box in range(3):
        spread_leaves(box)
    loads[5].wait()

    def far_step(c, carry):
        parts = []
        for l in range(child):
            tiles = []
            for t in range(k0 // fold):
                piece = leaf_tiles[far_source[c * child + l, t * fold] & (4 * leaves - 1)]
                for w in range(1, fold):
                    source = far_source[c * child + l, t * fold + w] & (4 * leaves - 1)
                    piece = jnp.where(lane_block == w, leaf_tiles[source], piece)
                tiles.append(piece)
            parts.append(jnp.concatenate(tiles, axis=1))
        lhs = jnp.concatenate(parts, axis=0).astype(BF16)
        matrix = far_coupling[pl.ds(c * child, child)].reshape(child * r0, k0 * r0)
        leaf_far[c] = diagonal(dot_nt(lhs, matrix), v, r0)
        return carry

    lax.fori_loop(0, groups, far_step, 0)

    halo_arrive(2)
    for box in range(3):
        spread_pairs(mw, mid_tiles, groups, box)
    loads[4].wait()
    for g in range(groups // quad):
        parts = []
        for c in range(g * quad, (g + 1) * quad):
            tiles = []
            for t in range(k1 // 2):
                a = mid_tiles[mid_source[c, 2 * t] & (4 * groups - 1)]
                b = mid_tiles[mid_source[c, 2 * t + 1] & (4 * groups - 1)]
                tiles.append(jnp.where(half, a, b))
            parts.append(jnp.concatenate(tiles, axis=1))
        lhs = jnp.concatenate(parts, axis=0).astype(BF16)
        matrix = mid_coupling[g * quad:(g + 1) * quad].reshape(quad * r, k1 * r)
        mid_far[:, g * quad * r:(g + 1) * quad * r] = diagonal(dot_nt(lhs, matrix), v, r)

    loads[6].wait()
    loads[7].wait()
    for copy in tops:
        copy.wait()

    def arrive_step(step, carry):
        arrival(lax.rem(me + step, n)).wait_recv()
        return carry

    lax.fori_loop(1, n, arrive_step, 0)

    offset = 0
    for level in range(levels):
        size = n >> level
        start = n - size
        below = gathered if level == 0 else upward
        for q in range(size // 2):
            a = below[offset + 2 * q]
            b = below[offset + 2 * q + 1]
            t = top_transfer[start + q]
            upward[start + q] = exact_nt(jnp.where(low_lane, a, b), jnp.concatenate([t, t], axis=0))
        offset = start
    across = []
    for level in range(levels + 1):
        size = n >> level
        cluster = me >> level
        below = gathered if level == 0 else upward
        base = 0 if level == 0 else n - (n >> (level - 1))
        odd = lax.rem(cluster, 2)
        found = []
        for partner in (cluster - 2 - odd, cluster + 2 - 4 * odd, cluster + 3 - odd):
            inside = (partner >= 0) & (partner < size)
            safe = jnp.clip(partner, 0, size - 1)
            found.append(below[base + safe] * jnp.where(inside, 1.0, 0.0))
        g = box_coupling[...] if level == 0 else top_coupling[level - 1]
        g = jnp.concatenate([g, g], axis=0)
        across.append(exact_nt(jnp.where(low_lane, found[0], found[1]), g[:, :2 * r])
                      + exact_nt(found[2][:, :r], g[:, 2 * r:]))
    downward = across[levels]
    for level in range(levels - 1, -1, -1):
        cluster = me >> level
        start = n - (n >> level)
        pushed = exact_nn(downward[:, :r], top_transfer[start + (cluster >> 1)])
        turned = pltpu.roll(pushed, LANES // 2, 1)
        left = jnp.where(low_lane, pushed, turned)
        right = jnp.where(low_lane, turned, pushed)
        odd = lax.rem(cluster, 2).astype(F32)
        downward = across[level] + left * (1.0 - odd) + right * odd

    mid_push = dot_nn(downward[:, :r].astype(BF16), mid_transfer[...])
    mid_down = (mid_far[...] + mid_push).astype(BF16).astype(F32)
    near_half = lanes((v, LANES)) < m
    for pair in range(groups // 2):
        tile = mid_down[:, pair * LANES:(pair + 1) * LANES]
        lhs = jnp.concatenate([jnp.where(low_lane, tile, 0.0), jnp.where(low_lane, 0.0, tile)], axis=0).astype(BF16)
        matrix = leaf_transfer[2 * pair:2 * pair + 2].reshape(2 * r, child * r0)
        push = dot_nn(lhs, matrix)
        for s in range(2):
            c = 2 * pair + s
            leaf_down = (leaf_far[c] + push[s * v:(s + 1) * v]).astype(BF16)
            for h in range(child // 4):
                q = c * (child // 4) + h
                far = dot_nn(leaf_down[:, h * 4 * r0:(h + 1) * 4 * r0], masked_basis[q])
                for w in range(2):
                    leaf = q * 4 + 2 * w
                    a = near_rows[pl.ds(leaf, v, stride=leaves), :]
                    b = near_rows[pl.ds(leaf + 1, v, stride=leaves), :]
                    a = a + pltpu.roll(a, m, 1)
                    b = b + pltpu.roll(b, m, 1)
                    near = jnp.where(near_half, a, b)
                    out_ref[:, leaf * m:(leaf + 2) * m] = (far[:, w * LANES:(w + 1) * LANES] + near).astype(BF16)

    def sent_step(step, carry):
        everyone(step).wait_send()
        return carry

    lax.fori_loop(1, n, sent_step, 0)
    for kind in range(3):
        halo_sent(kind)


def body(
    charges, leaf_basis, leaf_transfer, mid_transfer, far_source, far_coupling, mid_source, mid_coupling,
    box_coupling, top_transfer, top_coupling, near_target, near_source, near_count, near_blocks,
):
    n = lax.axis_size(AXIS)
    v, points = charges.shape
    leaves, k0 = far_source.shape
    m = points // leaves
    r0 = leaf_basis.shape[0]
    groups, k1 = mid_source.shape
    r = leaf_transfer.shape[1]
    capacity = near_target.shape[0]
    levels = (n // 4).bit_length() - 1
    sizes = (v, leaves, m, r0, groups, r, k0, k1, capacity)
    smem = pl.BlockSpec(memory_space=pltpu.SMEM)
    vmem = pl.BlockSpec(memory_space=pltpu.VMEM)
    hbm = pl.BlockSpec(memory_space=pl.ANY)
    dma = pltpu.SemaphoreType.DMA
    return pl.pallas_call(
        functools.partial(kernel, n, sizes),
        out_shape=jax.ShapeDtypeStruct(charges.shape, BF16),
        in_specs=[smem, smem, smem, smem, vmem] + [hbm] * 10,
        out_specs=vmem,
        scratch_shapes=[
            pltpu.VMEM((3, v, points), BF16),
            pltpu.VMEM((3, v, leaves * r0), BF16),
            pltpu.VMEM((3, v, groups * r), BF16),
            pltpu.VMEM((n, v, 2 * r), F32),
            pltpu.VMEM(leaf_basis.shape, BF16),
            pltpu.VMEM(leaf_transfer.shape, BF16),
            pltpu.VMEM(mid_transfer.shape[1:], BF16),
            pltpu.VMEM(far_coupling.shape, BF16),
            pltpu.VMEM(mid_coupling.shape, BF16),
            pltpu.VMEM(box_coupling.shape[1:], BF16),
            pltpu.VMEM(top_transfer.shape, BF16),
            pltpu.VMEM((levels,) + top_coupling.shape[1:], BF16),
            pltpu.VMEM(near_blocks.shape, BF16),
            pltpu.VMEM((4 * leaves, v, LANES), F32),
            pltpu.VMEM((4 * leaves, v, LANES), F32),
            pltpu.VMEM((4 * groups, v, LANES), F32),
            pltpu.VMEM((capacity * v, m), F32),
            pltpu.VMEM((v * leaves, 2 * m), F32),
            pltpu.VMEM((groups, v, leaves // groups * r0), F32),
            pltpu.VMEM((v, groups * r), F32),
            pltpu.VMEM((leaves // 4, 4 * r0, 4 * m), BF16),
            pltpu.VMEM((n, v, 2 * r), F32),
            dma((8,)),
            dma((CHUNKS,)),
            dma((levels,)),
            dma((6,)),
            dma((6,)),
            dma((n,)),
            dma((n,)),
        ],
        compiler_params=pltpu.CompilerParams(
            collective_id=0, has_side_effects=True, vmem_limit_bytes=60 * 1024 * 1024),
    )(
        near_source, far_source, mid_source, near_count, near_target.reshape(capacity // LANES, LANES),
        charges, leaf_basis, leaf_transfer, mid_transfer, far_coupling, mid_coupling,
        box_coupling, top_transfer, top_coupling, near_blocks,
    )


def solution(mesh):
    c = "clusters"
    in_specs = (
        P(None, c), P(None, c), P(c, None, None), P(c, None, None), P(c, None), P(c, None, None),
        P(c, None), P(c, None, None), P(c, None, None), P(), P(), P(c), P(c), P(c), P(None, c),
    )
    return jax.shard_map(body, mesh=mesh, in_specs=in_specs, out_specs=P(None, c), check_vma=False)
```

time: 237 us -> 31.1 us (0.13); the launches traced: 233 us -> 30.8 us
  local copies, waits for them, and re-layouts: 88.1 us -> 2.87 us
  starting transfers between devices: 70.7 us -> 0 us
  matrix products: 61.8 us -> 0 us
  Pallas kernels: 0 us -> 27.2 us
  other arithmetic: 11.7 us -> 0 us
    ppermute x25 -> x0, starting transfers between devices: 70.7 us -> none  [the longest x16 44.6 us: from_behind(): lax.ppermute(value, axis, [(source, source + steps) for source in range(i...]
    dot_general x32 -> x0, matrix products: 61.8 us -> none  [the longest x8 24 us: near_step(): jnp.einsum('tbs,vbs->vbt', dense, gathered, preferred_element_type=jnp.fl...]
    reshape x28 -> x0, local copies, waits for them, and re-layouts: 33.3 us -> none  [the longest x8 26.1 us: near_step(): dense = lax.dynamic_slice_in_dim(blocks, first * leaf_capacity, block * l...]
    gather x12 -> x0, local copies, waits for them, and re-layouts: 30 us -> none  [the longest x2 14.7 us: body(): picked = jnp.take(leaf_wide, offset, axis=0)]
    pallas_call x0 -> x1, Pallas kernels: none -> 27.2 us  [body(): pl.pallas_call(functools.partial(kernel, n, sizes), out_shape=jax.ShapeDt...]
    dynamic_slice x16 -> x0, local copies, waits for them, and re-layouts: 16.5 us -> none  [the longest x8 10.4 us: near_step(): lax.dynamic_slice_in_dim(blocks, first * leaf_capacity, block * leaf_capa...]
    and x10 -> x0, other arithmetic: 7.2 us -> none  [the longest x8 5.8 us: fetch_local(): jnp.take(wide_cube, lax.dynamic_slice_in_dim(local_source, first, block),...]
  transfers between devices with their start and end apart: 25 -> 0, of which waited for: 0 -> 0; matrix products, arithmetic and copies ran while one was open for 19% -> 0% of each run, Pallas kernels for 0% -> 0%
where the time goes in v1:
time: 31.1 us; the launch traced here: 30.8 us
  Pallas kernels  27.2 us (87%)
  local copies, waits for them, and re-layouts  2.87 us (9%)
  between operations  0.66 us (2%)
    pallas_call x1, Pallas kernels, body(): pl.pallas_call(functools.partial(kernel, n, sizes), out_shape=jax.ShapeDt...  27.2 us
    unnamed x2, local copies, waits for them, and re-layouts  2.87 us

profile of v1, /device:TPU:1, one launch (start us, length us, event | category | flops | bytes accessed | tf_op | source)
XLA Modules:
  0.0 30.8 jit_solution(15997503040712687433)
XLA Ops:
  0.7 1.4 %copy.16.far_source = s32[64,16]{1,0:T(8,128)} copy(s32[64,16]{0,1:T(8,128)} %param.19) | data formatting | bytes 8192 | tf_op args[4]
  2.0 27.2 %shard_map.145 = bf16[8,4096]{1,0:T(8,128)(2,1)} custom-call(s32[1024]{0:T(1024)} %near_source.1, s32[64,16]{1,0:T(8,128)} %copy.16.far_source, s32[8,8]{1,0:T(8,128)} %mid_source.1, s32[1]{0:T(128)S(6)} %copy.18.near_count, s32[8,128]{1,0:T(8,128)} %bitcast.1, bf16[8,4096]{1,0:T(8,128)(2,1)} %charges_h.1, bf16[32,4096]{1,0:T(8,128)(2,1)} %basis_h.1, ...), custom_call_target="tpu_custom_call" | custom-call | tf_op jit(solution)/shard_map/pallas_call | solution.py:423
  29.3 1.5 %copy.19 = bf16[8,4096]{1,0:T(8,128)(2,1)} copy(bf16[8,4096]{1,0:T(8,128)(2,1)} %shard_map.145) | data formatting | bytes 131072

commit v2 on v1

--- a/solution.py
+++ b/solution.py
@@ -66,7 +66,7 @@
     out_ref,
     cw, lw, mw, gathered, basis, leaf_transfer, mid_transfer, far_coupling, mid_coupling,
     box_coupling, top_transfer, top_coupling, near_blocks,
-    charge_tiles, leaf_tiles, mid_tiles, contribution, near_rows, leaf_far, mid_far, masked_basis, upward,
+    charge_tiles, leaf_tiles, mid_tiles, contribution, near_rows, leaf_far, mid_far, masked_basis, upward, assigned,
     load_sem, near_sem, top_sem, halo_send, halo_recv, all_send, all_recv,
 ):
     v, leaves, m, r0, groups, r, k0, k1, capacity = sizes
@@ -77,13 +77,6 @@
     low_lane = lanes((v, LANES)) < r
 
     barrier = pltpu.get_barrier_semaphore()
-
-    def greet(step, carry):
-        other = lax.rem(me + step, n)
-        pl.semaphore_signal(barrier, inc=1, device_id=(other,), device_id_type=pl.DeviceIdType.MESH)
-        return carry
-
-    lax.fori_loop(1, n, greet, 0)
 
     pairs = [
         (charges_h, cw.at[1]), (basis_h, basis), (leaf_transfer_h, leaf_transfer), (mid_transfer_h.at[0], mid_transfer),
@@ -110,6 +103,13 @@
             top_coupling_h.at[start + (me >> level)], top_coupling.at[level - 1], top_sem.at[level - 1]))
     for copy in tops:
         copy.start()
+
+    def greet(step, carry):
+        other = lax.rem(me + step, n)
+        pl.semaphore_signal(barrier, inc=1, device_id=(other,), device_id_type=pl.DeviceIdType.MESH)
+        return carry
+
+    lax.fori_loop(1, n, greet, 0)
 
     loads[0].wait()
     loads[1].wait()
@@ -134,75 +134,6 @@
     box_up = dot_nt(mw[1], jnp.concatenate([transfer, transfer], axis=0))
     gathered[me] = box_up
 
-    pl.semaphore_wait(barrier, n - 1)
-
-    def everyone(step):
-        other = lax.rem(me + step, n)
-        return pltpu.make_async_remote_copy(
-            src_ref=gathered.at[me], dst_ref=gathered.at[me], send_sem=all_send.at[step],
-            recv_sem=all_recv.at[me], device_id=(other,), device_id_type=pl.DeviceIdType.MESH)
-
-    def arrival(source):
-        return pltpu.make_async_remote_copy(
-            src_ref=gathered.at[source], dst_ref=gathered.at[source], send_sem=all_send.at[0],
-            recv_sem=all_recv.at[source], device_id=(me,), device_id_type=pl.DeviceIdType.MESH)
-
-    wides = (cw, lw, mw)
-
-    def halo(kind, side):
-        wide = wides[kind]
-        return pltpu.make_async_remote_copy(
-            src_ref=wide.at[1], dst_ref=wide.at[2 - 2 * side], send_sem=halo_send.at[2 * kind + side],
-            recv_sem=halo_recv.at[2 * kind + side], device_id=(me - 1 + 2 * side,),
-            device_id_type=pl.DeviceIdType.MESH)
-
-    def halo_starts(kind):
-        @pl.when(me > 0)
-        def _():
-            halo(kind, 0).start()
-
-        @pl.when(me < n - 1)
-        def _():
-            halo(kind, 1).start()
-
-    def halo_arrive(kind):
-        wide = wides[kind]
-
-        @pl.when(me < n - 1)
-        def _():
-            halo(kind, 0).wait_recv()
-
-        @pl.when(me > 0)
-        def _():
-            halo(kind, 1).wait_recv()
-
-        @pl.when(me == 0)
-        def _():
-            wide[0] = jnp.zeros(wide.shape[1:], BF16)
-
-        @pl.when(me == n - 1)
-        def _():
-            wide[2] = jnp.zeros(wide.shape[1:], BF16)
-
-    def halo_sent(kind):
-        @pl.when(me > 0)
-        def _():
-            halo(kind, 0).wait_send()
-
-        @pl.when(me < n - 1)
-        def _():
-            halo(kind, 1).wait_send()
-
-    halo_starts(0)
-
-    def send_step(step, carry):
-        everyone(step).start()
-        return carry
-
-    lax.fori_loop(1, n, send_step, 0)
-    halo_starts(1)
-    halo_starts(2)
-
     quad_mask = (rows((4 * r0, 4 * m)) // r0 == lanes((4 * r0, 4 * m)) // m).astype(F32).astype(BF16)
     for q in range(leaves // 4):
         b = basis[:, q * 4 * m:(q + 1) * 4 * m]
@@ -214,6 +145,9 @@
     for b in range(capacity // LANES):
         hit = (leaf_row == near_target[b:b + 1, :]) & (slot_lane + b * LANES < count)
         assignment.append(jnp.where(hit, 1.0, 0.0).astype(BF16))
+    assignment = [jnp.concatenate(assignment[b:b + 2], axis=1) for b in range(0, len(assignment), 2)]
+    for b, value in enumerate(assignment):
+        assigned[b] = value
 
     def spread_pairs(wide, tiles, per_box, box):
         x = wide[box].astype(F32)
@@ -243,47 +177,80 @@
         unused = pl.ds(lax.rem(me + 2, 4) * per_box, per_box)
         tiles[unused] = jnp.zeros((per_box, v, LANES), F32)
     spread_pairs(cw, charge_tiles, leaves, 1)
-    halo_arrive(0)
-    spread_pairs(cw, charge_tiles, leaves, 0)
-    spread_pairs(cw, charge_tiles, leaves, 2)
-
-    block = 32
-    zero = jnp.zeros((2 * v, LANES), F32)
-    steps_per_chunk = capacity // CHUNKS // block
-
-    def near_step(step, carry):
-        base = step * block
-        for g in range(block // 4):
-            pieces = []
-            for i in range(4):
-                x = charge_tiles[near_source[base + g * 4 + i] & (4 * leaves - 1)]
-                pieces.append(jnp.where(half, x, 0.0) if i % 2 == 0 else jnp.where(half, 0.0, x))
-            upper = jnp.concatenate([pieces[0], pieces[1]], axis=0)
-            lower = jnp.concatenate([pieces[2], pieces[3]], axis=0)
-            lhs = jnp.concatenate(
-                [jnp.concatenate([upper, zero], axis=1), jnp.concatenate([zero, lower], axis=1)], axis=0).astype(BF16)
-            span = pl.ds(pl.multiple_of(base * m + g * 4 * m, 4 * m), 4 * m)
-            contribution[pl.ds(pl.multiple_of((base + g * 4) * v, 4 * v), 4 * v), :] = dot_nt(lhs, near_blocks[:, span])
+    spread_leaves(1)
+    spread_pairs(mw, mid_tiles, groups, 1)
+
+    pl.semaphore_wait(barrier, n - 1)
+
+    def everyone(step):
+        other = lax.rem(me + step, n)
+        return pltpu.make_async_remote_copy(
+            src_ref=gathered.at[me], dst_ref=gathered.at[me], send_sem=all_send.at[step],
+            recv_sem=all_recv.at[me], device_id=(other,), device_id_type=pl.DeviceIdType.MESH)
+
+    def arrival(source):
+        return pltpu.make_async_remote_copy(
+            src_ref=gathered.at[source], dst_ref=gathered.at[source], send_sem=all_send.at[0],
+            recv_sem=all_recv.at[source], device_id=(me,), device_id_type=pl.DeviceIdType.MESH)
+
+    wides = (cw, lw, mw)
+
+    def halo(kind, side):
+        wide = wides[kind]
+        return pltpu.make_async_remote_copy(
+            src_ref=wide.at[1], dst_ref=wide.at[2 - 2 * side], send_sem=halo_send.at[2 * kind + side],
+            recv_sem=halo_recv.at[2 * kind + side], device_id=(me - 1 + 2 * side,),
+            device_id_type=pl.DeviceIdType.MESH)
+
+    def halo_starts(kind):
+        @pl.when(me > 0)
+        def _():
+            halo(kind, 0).start()
+
+        @pl.when(me < n - 1)
+        def _():
+            halo(kind, 1).start()
+
+    def halo_arrive(kind):
+        wide = wides[kind]
+
+        @pl.when(me < n - 1)
+        def _():
+            halo(kind, 0).wait_recv()
+
+        @pl.when(me > 0)
+        def _():
+            halo(kind, 1).wait_recv()
+
+        @pl.when(me == 0)
+        def _():
+            wide[0] = jnp.zeros(wide.shape[1:], BF16)
+
+        @pl.when(me == n - 1)
+        def _():
+            wide[2] = jnp.zeros(wide.shape[1:], BF16)
+
+    def halo_sent(kind):
+        @pl.when(me > 0)
+        def _():
+            halo(kind, 0).wait_send()
+
+        @pl.when(me < n - 1)
+        def _():
+            halo(kind, 1).wait_send()
+
+    def send_step(step, carry):
+        everyone(step).start()
         return carry
 
-    def near_chunk(chunk, carry):
-        near_load(chunk).wait()
-        return lax.fori_loop(chunk * steps_per_chunk, (chunk + 1) * steps_per_chunk, near_step, carry)
-
-    lax.fori_loop(0, CHUNKS, near_chunk, 0)
-
-    for u in range(v):
-        total = jnp.zeros((leaves, 2 * m), F32)
-        for b in range(capacity // LANES):
-            c = contribution[pl.ds(b * LANES * v + u, LANES, stride=v), :]
-            high = c.astype(BF16)
-            low = (c - high.astype(F32)).astype(BF16)
-            total = total + dot_nn(assignment[b], jnp.concatenate([high, low], axis=1))
-        near_rows[u * leaves:(u + 1) * leaves, :] = total
+    halo_starts(1)
+    halo_starts(0)
+    halo_starts(2)
+    lax.fori_loop(1, n, send_step, 0)
 
     halo_arrive(1)
-    for box in range(3):
-        spread_leaves(box)
+    spread_leaves(0)
+    spread_leaves(2)
     loads[5].wait()
 
     def far_step(c, carry):
@@ -291,22 +258,49 @@
         for l in range(child):
             tiles = []
             for t in range(k0 // fold):
-                piece = leaf_tiles[far_source[c * child + l, t * fold] & (4 * leaves - 1)]
+                piece = leaf_tiles[far_source[t * fold, c * child + l] & (4 * leaves - 1)]
                 for w in range(1, fold):
-                    source = far_source[c * child + l, t * fold + w] & (4 * leaves - 1)
+                    source = far_source[t * fold + w, c * child + l] & (4 * leaves - 1)
                     piece = jnp.where(lane_block == w, leaf_tiles[source], piece)
                 tiles.append(piece)
             parts.append(jnp.concatenate(tiles, axis=1))
         lhs = jnp.concatenate(parts, axis=0).astype(BF16)
-        matrix = far_coupling[pl.ds(c * child, child)].reshape(child * r0, k0 * r0)
+        matrix = far_coupling[c * child:(c + 1) * child].reshape(child * r0, k0 * r0)
         leaf_far[c] = diagonal(dot_nt(lhs, matrix), v, r0)
         return carry
 
-    lax.fori_loop(0, groups, far_step, 0)
+    for c in range(groups):
+        far_step(c, 0)
+
+    halo_arrive(0)
+    spread_pairs(cw, charge_tiles, leaves, 0)
+    spread_pairs(cw, charge_tiles, leaves, 2)
+
+    zero = jnp.zeros((2 * v, LANES), F32)
+
+    for g in range(capacity // 4):
+        if g % (capacity // 4 // CHUNKS) == 0:
+            near_load(g // (capacity // 4 // CHUNKS)).wait()
+        pieces = []
+        for i in range(4):
+            x = charge_tiles[near_source[g * 4 + i] & (4 * leaves - 1)]
+            pieces.append(jnp.where(half, x, 0.0) if i % 2 == 0 else jnp.where(half, 0.0, x))
+        upper = jnp.concatenate([pieces[0], pieces[1]], axis=0)
+        lower = jnp.concatenate([pieces[2], pieces[3]], axis=0)
+        lhs = jnp.concatenate(
+            [jnp.concatenate([upper, zero], axis=1), jnp.concatenate([zero, lower], axis=1)], axis=0).astype(BF16)
+        contribution[g * 4 * v:(g + 1) * 4 * v, :] = dot_nt(lhs, near_blocks[:, g * 4 * m:(g + 1) * 4 * m])
+
+    for u in range(v):
+        total = jnp.zeros((leaves, m), F32)
+        for b in range(capacity // LANES // 2):
+            c = contribution[pl.ds(b * 2 * LANES * v + u, 2 * LANES, stride=v), :]
+            total = total + dot_nn(assigned[b], c.astype(BF16))
+        near_rows[u * leaves:(u + 1) * leaves, :] = jnp.concatenate([total, total], axis=1)
 
     halo_arrive(2)
-    for box in range(3):
-        spread_pairs(mw, mid_tiles, groups, box)
+    spread_pairs(mw, mid_tiles, groups, 0)
+    spread_pairs(mw, mid_tiles, groups, 2)
     loads[4].wait()
     for g in range(groups // quad):
         parts = []
@@ -388,8 +382,6 @@
                     leaf = q * 4 + 2 * w
                     a = near_rows[pl.ds(leaf, v, stride=leaves), :]
                     b = near_rows[pl.ds(leaf + 1, v, stride=leaves), :]
-                    a = a + pltpu.roll(a, m, 1)
-                    b = b + pltpu.roll(b, m, 1)
                     near = jnp.where(near_half, a, b)
                     out_ref[:, leaf * m:(leaf + 2) * m] = (far[:, w * LANES:(w + 1) * LANES] + near).astype(BF16)
 
@@ -448,6 +440,7 @@
             pltpu.VMEM((v, groups * r), F32),
             pltpu.VMEM((leaves // 4, 4 * r0, 4 * m), BF16),
             pltpu.VMEM((n, v, 2 * r), F32),
+            pltpu.VMEM((capacity // LANES // 2, leaves, 2 * LANES), BF16),
             dma((8,)),
             dma((CHUNKS,)),
             dma((levels,)),
@@ -459,7 +452,7 @@
         compiler_params=pltpu.CompilerParams(
             collective_id=0, has_side_effects=True, vmem_limit_bytes=60 * 1024 * 1024),
     )(
-        near_source, far_source, mid_source, near_count, near_target.reshape(capacity // LANES, LANES),
+        near_source, far_source.T, mid_source, near_count, near_target.reshape(capacity // LANES, LANES),
         charges, leaf_basis, leaf_transfer, mid_transfer, far_coupling, mid_coupling,
         box_coupling, top_transfer, top_coupling, near_blocks,
     )

time: 31.1 us -> 23.9 us (0.77)
  Pallas kernels: 27.2 us -> 21.6 us
  local copies, waits for them, and re-layouts: 2.87 us -> 1.47 us
    pallas_call x1, Pallas kernels: 27.2 us -> 21.6 us  [body(): pl.pallas_call(functools.partial(kernel, n, sizes), out_shape=jax.ShapeDt...]
    unnamed x2 -> x1, local copies, waits for them, and re-layouts: 2.87 us -> 1.47 us
where the time goes in v2:
time: 23.9 us; the launch traced here: 23.7 us
  Pallas kernels  21.6 us (90%)
  local copies, waits for them, and re-layouts  1.47 us (6%)
  between operations  0.66 us (3%)
    pallas_call x1, Pallas kernels, body(): pl.pallas_call(functools.partial(kernel, n, sizes), out_shape=jax.ShapeDt...  21.6 us
    unnamed x1, local copies, waits for them, and re-layouts  1.47 us

profile of v2, /device:TPU:1, one launch (start us, length us, event | category | flops | bytes accessed | tf_op | source)
XLA Modules:
  0.0 23.7 jit_solution(9391998593984148124)
XLA Ops:
  0.7 21.6 %shard_map.145 = bf16[8,4096]{1,0:T(8,128)(2,1)} custom-call(s32[1024]{0:T(1024)} %near_source.1, s32[16,64]{1,0:T(8,128)} %bitcast.2, s32[8,8]{1,0:T(8,128)} %mid_source.1, s32[1]{0:T(128)S(6)} %copy.17.near_count, s32[8,128]{1,0:T(8,128)} %bitcast.3, bf16[8,4096]{1,0:T(8,128)(2,1)} %charges_h.1, bf16[32,4096]{1,0:T(8,128)(2,1)} %basis_h.1, ...), custom_call_target="tpu_custom_call" | custom-call | tf_op jit(solution)/shard_map/pallas_call | solution.py:415
  22.3 1.5 %copy.18 = bf16[8,4096]{1,0:T(8,128)(2,1)} copy(bf16[8,4096]{1,0:T(8,128)(2,1)} %shard_map.145) | data formatting | bytes 131072

commit v3 on v2

--- a/solution.py
+++ b/solution.py
@@ -104,12 +104,22 @@
     for copy in tops:
         copy.start()
 
-    def greet(step, carry):
-        other = lax.rem(me + step, n)
-        pl.semaphore_signal(barrier, inc=1, device_id=(other,), device_id_type=pl.DeviceIdType.MESH)
-        return carry
-
-    lax.fori_loop(1, n, greet, 0)
+    mesh_id = pl.DeviceIdType.MESH
+    rounds = (n - 1).bit_length()
+    odd_me = lax.rem(me, 2)
+    outer = me - 1 + 2 * odd_me
+    has_outer = (outer >= 0) & (outer < n)
+
+    def partner(k):
+        bit = lax.rem(me >> k, 2)
+        return me + (1 << k) * (1 - 2 * bit)
+
+    @pl.when(has_outer)
+    def _():
+        pl.semaphore_signal(barrier, inc=1, device_id=(outer,), device_id_type=mesh_id)
+
+    for k in range(rounds):
+        pl.semaphore_signal(barrier, inc=1, device_id=(partner(k),), device_id_type=mesh_id)
 
     loads[0].wait()
     loads[1].wait()
@@ -145,7 +155,8 @@
     for b in range(capacity // LANES):
         hit = (leaf_row == near_target[b:b + 1, :]) & (slot_lane + b * LANES < count)
         assignment.append(jnp.where(hit, 1.0, 0.0).astype(BF16))
-    assignment = [jnp.concatenate(assignment[b:b + 2], axis=1) for b in range(0, len(assignment), 2)]
+    per = len(assignment) // 4
+    assignment = [jnp.concatenate(assignment[b * per:(b + 1) * per], axis=1) for b in range(4)]
     for b, value in enumerate(assignment):
         assigned[b] = value
 
@@ -180,18 +191,32 @@
     spread_leaves(1)
     spread_pairs(mw, mid_tiles, groups, 1)
 
-    pl.semaphore_wait(barrier, n - 1)
-
-    def everyone(step):
-        other = lax.rem(me + step, n)
+    @pl.when(has_outer)
+    def _():
+        pl.semaphore_wait(barrier, rounds + 1)
+
+    @pl.when(jnp.logical_not(has_outer))
+    def _():
+        pl.semaphore_wait(barrier, rounds)
+
+    def exchange(k):
+        group = pl.ds((me >> k) << k, 1 << k)
         return pltpu.make_async_remote_copy(
-            src_ref=gathered.at[me], dst_ref=gathered.at[me], send_sem=all_send.at[step],
-            recv_sem=all_recv.at[me], device_id=(other,), device_id_type=pl.DeviceIdType.MESH)
-
-    def arrival(source):
-        return pltpu.make_async_remote_copy(
-            src_ref=gathered.at[source], dst_ref=gathered.at[source], send_sem=all_send.at[0],
-            recv_sem=all_recv.at[source], device_id=(me,), device_id_type=pl.DeviceIdType.MESH)
+            src_ref=gathered.at[group], dst_ref=gathered.at[group], send_sem=all_send.at[k],
+            recv_sem=all_recv.at[k], device_id=(partner(k),), device_id_type=mesh_id)
+
+    sent = []
+
+    def next_round():
+        k = len(sent)
+        if k > 0 and k <= rounds:
+            sent[k - 1].wait_recv()
+        if k < rounds:
+            copy = exchange(k)
+            copy.start()
+            sent.append(copy)
+        elif k == rounds:
+            sent.append(None)
 
     wides = (cw, lw, mw)
 
@@ -239,14 +264,10 @@
         def _():
             halo(kind, 1).wait_send()
 
-    def send_step(step, carry):
-        everyone(step).start()
-        return carry
-
+    next_round()
     halo_starts(1)
     halo_starts(0)
     halo_starts(2)
-    lax.fori_loop(1, n, send_step, 0)
 
     halo_arrive(1)
     spread_leaves(0)
@@ -269,34 +290,57 @@
         leaf_far[c] = diagonal(dot_nt(lhs, matrix), v, r0)
         return carry
 
+    next_round()
     for c in range(groups):
         far_step(c, 0)
+        if c % 4 == 3:
+            next_round()
 
     halo_arrive(0)
     spread_pairs(cw, charge_tiles, leaves, 0)
     spread_pairs(cw, charge_tiles, leaves, 2)
 
     zero = jnp.zeros((2 * v, LANES), F32)
-
-    for g in range(capacity // 4):
-        if g % (capacity // 4 // CHUNKS) == 0:
-            near_load(g // (capacity // 4 // CHUNKS)).wait()
-        pieces = []
-        for i in range(4):
-            x = charge_tiles[near_source[g * 4 + i] & (4 * leaves - 1)]
-            pieces.append(jnp.where(half, x, 0.0) if i % 2 == 0 else jnp.where(half, 0.0, x))
-        upper = jnp.concatenate([pieces[0], pieces[1]], axis=0)
-        lower = jnp.concatenate([pieces[2], pieces[3]], axis=0)
-        lhs = jnp.concatenate(
-            [jnp.concatenate([upper, zero], axis=1), jnp.concatenate([zero, lower], axis=1)], axis=0).astype(BF16)
-        contribution[g * 4 * v:(g + 1) * 4 * v, :] = dot_nt(lhs, near_blocks[:, g * 4 * m:(g + 1) * 4 * m])
-
+    wide_half = lanes((4 * v, LANES)) < m
+
+    for chunk in range(CHUNKS):
+        near_load(chunk).wait()
+    parts = 4
+    quarter = capacity // parts
+    for g in range(quarter // 4):
+        stacked = []
+        matrices = []
+        for h in range(parts):
+            first = h * quarter + g * 4
+            pieces = []
+            for i in range(4):
+                x = charge_tiles[near_source[first + i] & (4 * leaves - 1)]
+                pieces.append(jnp.where(half, x, 0.0) if i % 2 == 0 else jnp.where(half, 0.0, x))
+            upper = jnp.concatenate([pieces[0], pieces[1]], axis=0)
+            lower = jnp.concatenate([pieces[2], pieces[3]], axis=0)
+            stacked += [jnp.concatenate([upper, zero], axis=1), jnp.concatenate([zero, lower], axis=1)]
+            matrices.append(near_blocks[:, first * m:(first + 4) * m])
+        out = dot_nt(jnp.concatenate(stacked, axis=0).astype(BF16), jnp.concatenate(matrices, axis=0))
+        q = 4 * v
+        for w in range(2):
+            a = out[2 * w * q:(2 * w + 1) * q, w * LANES:(w + 1) * LANES]
+            b = out[(2 * w + 1) * q:(2 * w + 2) * q, w * LANES:(w + 1) * LANES]
+            contribution[w, g * q:(g + 1) * q, :] = jnp.where(wide_half, a, b)
+        if g in (quarter // 16, quarter // 8, 3 * quarter // 16):
+            next_round()
+
+    hits = assigned[...].reshape(parts * leaves, quarter)
+    tall_half = lanes((leaves, LANES)) < m
     for u in range(v):
-        total = jnp.zeros((leaves, m), F32)
-        for b in range(capacity // LANES // 2):
-            c = contribution[pl.ds(b * 2 * LANES * v + u, 2 * LANES, stride=v), :]
-            total = total + dot_nn(assigned[b], c.astype(BF16))
-        near_rows[u * leaves:(u + 1) * leaves, :] = jnp.concatenate([total, total], axis=1)
+        c = jnp.concatenate(
+            [contribution[w, pl.ds(u, quarter, stride=v), :] for w in range(2)], axis=1).astype(BF16)
+        out = dot_nn(hits, c)
+        total = jnp.zeros((leaves, LANES), F32)
+        for w in range(2):
+            a = out[2 * w * leaves:(2 * w + 1) * leaves, w * LANES:(w + 1) * LANES]
+            b = out[(2 * w + 1) * leaves:(2 * w + 2) * leaves, w * LANES:(w + 1) * LANES]
+            total = total + jnp.where(tall_half, a, b)
+        near_rows[u * leaves:(u + 1) * leaves, :] = total + pltpu.roll(total, m, 1)
 
     halo_arrive(2)
     spread_pairs(mw, mid_tiles, groups, 0)
@@ -320,11 +364,8 @@
     for copy in tops:
         copy.wait()
 
-    def arrive_step(step, carry):
-        arrival(lax.rem(me + step, n)).wait_recv()
-        return carry
-
-    lax.fori_loop(1, n, arrive_step, 0)
+    while len(sent) <= rounds:
+        next_round()
 
     offset = 0
     for level in range(levels):
@@ -385,11 +426,8 @@
                     near = jnp.where(near_half, a, b)
                     out_ref[:, leaf * m:(leaf + 2) * m] = (far[:, w * LANES:(w + 1) * LANES] + near).astype(BF16)
 
-    def sent_step(step, carry):
-        everyone(step).wait_send()
-        return carry
-
-    lax.fori_loop(1, n, sent_step, 0)
+    for copy in sent[:rounds]:
+        copy.wait_send()
     for kind in range(3):
         halo_sent(kind)
 
@@ -434,20 +472,20 @@
             pltpu.VMEM((4 * leaves, v, LANES), F32),
             pltpu.VMEM((4 * leaves, v, LANES), F32),
             pltpu.VMEM((4 * groups, v, LANES), F32),
-            pltpu.VMEM((capacity * v, m), F32),
+            pltpu.VMEM((2, capacity // 4 * v, LANES), F32),
             pltpu.VMEM((v * leaves, 2 * m), F32),
             pltpu.VMEM((groups, v, leaves // groups * r0), F32),
             pltpu.VMEM((v, groups * r), F32),
             pltpu.VMEM((leaves // 4, 4 * r0, 4 * m), BF16),
             pltpu.VMEM((n, v, 2 * r), F32),
-            pltpu.VMEM((capacity // LANES // 2, leaves, 2 * LANES), BF16),
+            pltpu.VMEM((4, leaves, capacity // 4), BF16),
             dma((8,)),
             dma((CHUNKS,)),
             dma((levels,)),
             dma((6,)),
             dma((6,)),
-            dma((n,)),
-            dma((n,)),
+            dma(((n - 1).bit_length(),)),
+            dma(((n - 1).bit_length(),)),
         ],
         compiler_params=pltpu.CompilerParams(
             collective_id=0, has_side_effects=True, vmem_limit_bytes=60 * 1024 * 1024),

time: 23.9 us -> 30.2 us (1.26)
  the two profiles are of different devices: /device:TPU:1 before, /device:TPU:0 now
where the time goes in v3:
time: 30.2 us; the launch traced here: 29.9 us
  Pallas kernels  27.8 us (92%)
  local copies, waits for them, and re-layouts  1.47 us (5%)
  between operations  0.66 us (2%)
    pallas_call x1, Pallas kernels, body(): pl.pallas_call(functools.partial(kernel, n, sizes), out_shape=jax.ShapeDt...  27.8 us
    unnamed x1, local copies, waits for them, and re-layouts  1.47 us

profile of v3, /device:TPU:0, one launch (start us, length us, event | category | flops | bytes accessed | tf_op | source)
XLA Modules:
  0.0 29.9 jit_solution(14392136570476309090)
XLA Ops:
  0.7 27.8 %shard_map.145 = bf16[8,4096]{1,0:T(8,128)(2,1)} custom-call(s32[1024]{0:T(1024)} %near_source.1, s32[16,64]{1,0:T(8,128)} %bitcast.2, s32[8,8]{1,0:T(8,128)} %mid_source.1, s32[1]{0:T(128)S(6)} %copy.17.near_count, s32[8,128]{1,0:T(8,128)} %bitcast.3, bf16[8,4096]{1,0:T(8,128)(2,1)} %charges_h.1, bf16[32,4096]{1,0:T(8,128)(2,1)} %basis_h.1, ...), custom_call_target="tpu_custom_call" | custom-call | tf_op jit(solution)/shard_map/pallas_call | solution.py:453
  28.5 1.5 %copy.18 = bf16[8,4096]{1,0:T(8,128)(2,1)} copy(bf16[8,4096]{1,0:T(8,128)(2,1)} %shard_map.145) | data formatting | bytes 131072

commit v4 on v2

--- a/solution.py
+++ b/solution.py
@@ -61,7 +61,7 @@
 def kernel(
     n, sizes,
     near_source, far_source, mid_source, near_count, near_target,
-    charges_h, basis_h, leaf_transfer_h, mid_transfer_h, far_coupling_h, mid_coupling_h,
+    left_ref, right_ref, charges_h, basis_h, leaf_transfer_h, mid_transfer_h, far_coupling_h, mid_coupling_h,
     box_coupling_h, top_transfer_h, top_coupling_h, near_blocks_h,
     out_ref,
     cw, lw, mw, gathered, basis, leaf_transfer, mid_transfer, far_coupling, mid_coupling,
@@ -145,12 +145,16 @@
     for b in range(capacity // LANES):
         hit = (leaf_row == near_target[b:b + 1, :]) & (slot_lane + b * LANES < count)
         assignment.append(jnp.where(hit, 1.0, 0.0).astype(BF16))
-    assignment = [jnp.concatenate(assignment[b:b + 2], axis=1) for b in range(0, len(assignment), 2)]
+    per = len(assignment) // 4
+    assignment = [jnp.concatenate(assignment[b * per:(b + 1) * per], axis=1) for b in range(4)]
     for b, value in enumerate(assignment):
         assigned[b] = value
 
+    charge_boxes = (left_ref, cw.at[1], right_ref)
+    mid_boxes = tuple(mw.at[box] for box in range(3))
+
     def spread_pairs(wide, tiles, per_box, box):
-        x = wide[box].astype(F32)
+        x = wide[box][...].astype(F32)
         first = lax.rem(me + 3 + box, 4) * per_box
         for t in range(per_box // 2):
             tile = x[:, t * LANES:(t + 1) * LANES]
@@ -176,11 +180,9 @@
     for tiles, per_box in ((charge_tiles, leaves), (leaf_tiles, leaves), (mid_tiles, groups)):
         unused = pl.ds(lax.rem(me + 2, 4) * per_box, per_box)
         tiles[unused] = jnp.zeros((per_box, v, LANES), F32)
-    spread_pairs(cw, charge_tiles, leaves, 1)
+    spread_pairs(charge_boxes, charge_tiles, leaves, 1)
     spread_leaves(1)
-    spread_pairs(mw, mid_tiles, groups, 1)
-
-    pl.semaphore_wait(barrier, n - 1)
+    spread_pairs(mid_boxes, mid_tiles, groups, 1)
 
     def everyone(step):
         other = lax.rem(me + step, n)
@@ -193,7 +195,7 @@
             src_ref=gathered.at[source], dst_ref=gathered.at[source], send_sem=all_send.at[0],
             recv_sem=all_recv.at[source], device_id=(me,), device_id_type=pl.DeviceIdType.MESH)
 
-    wides = (cw, lw, mw)
+    wides = (lw, mw)
 
     def halo(kind, side):
         wide = wides[kind]
@@ -243,12 +245,55 @@
         everyone(step).start()
         return carry
 
-    halo_starts(1)
-    halo_starts(0)
-    halo_starts(2)
-    lax.fori_loop(1, n, send_step, 0)
-
-    halo_arrive(1)
+    spread_pairs(charge_boxes, charge_tiles, leaves, 0)
+    spread_pairs(charge_boxes, charge_tiles, leaves, 2)
+
+    zero = jnp.zeros((2 * v, LANES), F32)
+    wide_half = lanes((4 * v, LANES)) < m
+
+    for chunk in range(CHUNKS):
+        near_load(chunk).wait()
+    parts = 4
+    quarter = capacity // parts
+    for g in range(quarter // 4):
+        stacked = []
+        matrices = []
+        for h in range(parts):
+            first = h * quarter + g * 4
+            pieces = []
+            for i in range(4):
+                x = charge_tiles[near_source[first + i] & (4 * leaves - 1)]
+                pieces.append(jnp.where(half, x, 0.0) if i % 2 == 0 else jnp.where(half, 0.0, x))
+            upper = jnp.concatenate([pieces[0], pieces[1]], axis=0)
+            lower = jnp.concatenate([pieces[2], pieces[3]], axis=0)
+            stacked += [jnp.concatenate([upper, zero], axis=1), jnp.concatenate([zero, lower], axis=1)]
+            matrices.append(near_blocks[:, first * m:(first + 4) * m])
+        out = dot_nt(jnp.concatenate(stacked, axis=0).astype(BF16), jnp.concatenate(matrices, axis=0))
+        q = 4 * v
+        for w in range(2):
+            a = out[2 * w * q:(2 * w + 1) * q, w * LANES:(w + 1) * LANES]
+            b = out[(2 * w + 1) * q:(2 * w + 2) * q, w * LANES:(w + 1) * LANES]
+            contribution[w, g * q:(g + 1) * q, :] = jnp.where(wide_half, a, b)
+        if g == quarter // 8:
+            pl.semaphore_wait(barrier, n - 1)
+            halo_starts(0)
+            halo_starts(1)
+            lax.fori_loop(1, n, send_step, 0)
+
+    hits = assigned[...].reshape(parts * leaves, quarter)
+    tall_half = lanes((leaves, LANES)) < m
+    for u in range(v):
+        c = jnp.concatenate(
+            [contribution[w, pl.ds(u, quarter, stride=v), :] for w in range(2)], axis=1).astype(BF16)
+        out = dot_nn(hits, c)
+        total = jnp.zeros((leaves, LANES), F32)
+        for w in range(2):
+            a = out[2 * w * leaves:(2 * w + 1) * leaves, w * LANES:(w + 1) * LANES]
+            b = out[(2 * w + 1) * leaves:(2 * w + 2) * leaves, w * LANES:(w + 1) * LANES]
+            total = total + jnp.where(tall_half, a, b)
+        near_rows[u * leaves:(u + 1) * leaves, :] = total + pltpu.roll(total, m, 1)
+
+    halo_arrive(0)
     spread_leaves(0)
     spread_leaves(2)
     loads[5].wait()
@@ -272,35 +317,9 @@
     for c in range(groups):
         far_step(c, 0)
 
-    halo_arrive(0)
-    spread_pairs(cw, charge_tiles, leaves, 0)
-    spread_pairs(cw, charge_tiles, leaves, 2)
-
-    zero = jnp.zeros((2 * v, LANES), F32)
-
-    for g in range(capacity // 4):
-        if g % (capacity // 4 // CHUNKS) == 0:
-            near_load(g // (capacity // 4 // CHUNKS)).wait()
-        pieces = []
-        for i in range(4):
-            x = charge_tiles[near_source[g * 4 + i] & (4 * leaves - 1)]
-            pieces.append(jnp.where(half, x, 0.0) if i % 2 == 0 else jnp.where(half, 0.0, x))
-        upper = jnp.concatenate([pieces[0], pieces[1]], axis=0)
-        lower = jnp.concatenate([pieces[2], pieces[3]], axis=0)
-        lhs = jnp.concatenate(
-            [jnp.concatenate([upper, zero], axis=1), jnp.concatenate([zero, lower], axis=1)], axis=0).astype(BF16)
-        contribution[g * 4 * v:(g + 1) * 4 * v, :] = dot_nt(lhs, near_blocks[:, g * 4 * m:(g + 1) * 4 * m])
-
-    for u in range(v):
-        total = jnp.zeros((leaves, m), F32)
-        for b in range(capacity // LANES // 2):
-            c = contribution[pl.ds(b * 2 * LANES * v + u, 2 * LANES, stride=v), :]
-            total = total + dot_nn(assigned[b], c.astype(BF16))
-        near_rows[u * leaves:(u + 1) * leaves, :] = jnp.concatenate([total, total], axis=1)
-
-    halo_arrive(2)
-    spread_pairs(mw, mid_tiles, groups, 0)
-    spread_pairs(mw, mid_tiles, groups, 2)
+    halo_arrive(1)
+    spread_pairs(mid_boxes, mid_tiles, groups, 0)
+    spread_pairs(mid_boxes, mid_tiles, groups, 2)
     loads[4].wait()
     for g in range(groups // quad):
         parts = []
@@ -390,7 +409,7 @@
         return carry
 
     lax.fori_loop(1, n, sent_step, 0)
-    for kind in range(3):
+    for kind in range(2):
         halo_sent(kind)
 
 
@@ -407,6 +426,8 @@
     r = leaf_transfer.shape[1]
     capacity = near_target.shape[0]
     levels = (n // 4).bit_length() - 1
+    left = lax.ppermute(charges, AXIS, [(i, i + 1) for i in range(n - 1)])
+    right = lax.ppermute(charges, AXIS, [(i + 1, i) for i in range(n - 1)])
     sizes = (v, leaves, m, r0, groups, r, k0, k1, capacity)
     smem = pl.BlockSpec(memory_space=pltpu.SMEM)
     vmem = pl.BlockSpec(memory_space=pltpu.VMEM)
@@ -415,7 +436,7 @@
     return pl.pallas_call(
         functools.partial(kernel, n, sizes),
         out_shape=jax.ShapeDtypeStruct(charges.shape, BF16),
-        in_specs=[smem, smem, smem, smem, vmem] + [hbm] * 10,
+        in_specs=[smem, smem, smem, smem, vmem, vmem, vmem] + [hbm] * 10,
         out_specs=vmem,
         scratch_shapes=[
             pltpu.VMEM((3, v, points), BF16),
@@ -434,18 +455,18 @@
             pltpu.VMEM((4 * leaves, v, LANES), F32),
             pltpu.VMEM((4 * leaves, v, LANES), F32),
             pltpu.VMEM((4 * groups, v, LANES), F32),
-            pltpu.VMEM((capacity * v, m), F32),
+            pltpu.VMEM((2, capacity // 4 * v, LANES), F32),
             pltpu.VMEM((v * leaves, 2 * m), F32),
             pltpu.VMEM((groups, v, leaves // groups * r0), F32),
             pltpu.VMEM((v, groups * r), F32),
             pltpu.VMEM((leaves // 4, 4 * r0, 4 * m), BF16),
             pltpu.VMEM((n, v, 2 * r), F32),
-            pltpu.VMEM((capacity // LANES // 2, leaves, 2 * LANES), BF16),
-            dma((8,)),
+            pltpu.VMEM((4, leaves, capacity // 4), BF16),
+            dma((10,)),
             dma((CHUNKS,)),
             dma((levels,)),
-            dma((6,)),
-            dma((6,)),
+            dma((4,)),
+            dma((4,)),
             dma((n,)),
             dma((n,)),
         ],
@@ -453,7 +474,7 @@
             collective_id=0, has_side_effects=True, vmem_limit_bytes=60 * 1024 * 1024),
     )(
         near_source, far_source.T, mid_source, near_count, near_target.reshape(capacity // LANES, LANES),
-        charges, leaf_basis, leaf_transfer, mid_transfer, far_coupling, mid_coupling,
+        left, right, charges, leaf_basis, leaf_transfer, mid_transfer, far_coupling, mid_coupling,
         box_coupling, top_transfer, top_coupling, near_blocks,
     )
 

time: 23.9 us -> 31.3 us (1.31)
  the two profiles are of different devices: /device:TPU:1 before, /device:TPU:0 now
where the time goes in v4:
time: 31.3 us; the launch traced here: 31 us
  Pallas kernels  21.1 us (67%)
  starting transfers between devices  3.68 us (12%)
  waiting for transfers between devices  3.49 us (11%)
  local copies, waits for them, and re-layouts  2.09 us (7%)
  between operations  0.69 us (2%)
    pallas_call x1, Pallas kernels, body(): pl.pallas_call(functools.partial(kernel, n, sizes), out_shape=jax.ShapeDt...  21.1 us
    ppermute x1, waiting for transfers between devices, body(): right = lax.ppermute(charges, AXIS, [(i + 1, i) for i in range(n - 1)])  3.48 us
    ppermute x1, starting transfers between devices, body(): left = lax.ppermute(charges, AXIS, [(i, i + 1) for i in range(n - 1)])  2.39 us
    unnamed x5, local copies, waits for them, and re-layouts  2.09 us
    ppermute x1, starting transfers between devices, body(): right = lax.ppermute(charges, AXIS, [(i + 1, i) for i in range(n - 1)])  1.29 us
  transfers between devices with their start and end apart: 2, of which 1 were waited for; matrix products, arithmetic and copies ran while one was open for 0% of the time, Pallas kernels for 0%

profile of v4, /device:TPU:0, one launch (start us, length us, event | category | flops | bytes accessed | tf_op | source)
XLA Modules:
  0.0 31.0 jit_solution(974369689271471606)
XLA Ops:
  0.0 2.4 %collective-permute-start = (bf16[8,4096]{1,0:T(8,128)(2,1)}, bf16[8,4096]{1,0:T(8,128)(2,1)S(1)}, u32[]{:S(2)}, u32[]{:S(2)}) collective-permute-start(bf16[8,4096]{1,0:T(8,128)(2,1)} %charges_h.1), channel_id=1, source_target_pairs={{0,1},{1,2},{2,3},{3,4},{4,5},{5,6},{6,7},{7,8},{8,9},{9,10},{10,1... | collective-permute-start | bytes 196616 | tf_op jit(solution)/shard_map/ppermute | solution.py:429
  2.4 1.3 %collective-permute-start.1 = (bf16[8,4096]{1,0:T(8,128)(2,1)}, bf16[8,4096]{1,0:T(8,128)(2,1)S(1)}, u32[]{:S(2)}, u32[]{:S(2)}) collective-permute-start(bf16[8,4096]{1,0:T(8,128)(2,1)} %charges_h.1), channel_id=1, source_target_pairs={{1,0},{2,1},{3,2},{4,3},{5,4},{6,5},{7,6},{8,7},{9,8},{10,9},{11,1... | collective-permute-start | bytes 196616 | tf_op jit(solution)/shard_map/ppermute | solution.py:430
  4.3 0.0 collective-permute-done.left_ref
  4.4 0.0 copy-start
  4.4 3.5 %collective-permute-done.1.right_ref = bf16[8,4096]{1,0:T(8,128)(2,1)S(1)} collective-permute-done((bf16[8,4096]{1,0:T(8,128)(2,1)}, bf16[8,4096]{1,0:T(8,128)(2,1)S(1)}, u32[]{:S(2)}, u32[]{:S(2)}) %collective-permute-start.1) | collective-permute-done | bytes 65568 | tf_op jit(solution)/shard_map/ppermute | solution.py:430
  7.8 0.0 copy-start.1
  7.8 0.0 copy-done
  7.9 0.6 %copy-done.1 = bf16[8,4096]{1,0:T(8,128)(2,1)} copy-done((bf16[8,4096]{1,0:T(8,128)(2,1)}, bf16[8,4096]{1,0:T(8,128)(2,1)S(1)}, u32[]{:S(2)}) %copy-start.1) | copy-done | bytes 65560
  8.5 21.1 %shard_map.145 = bf16[8,4096]{1,0:T(8,128)(2,1)} custom-call(s32[1024]{0:T(1024)} %near_source.1, s32[16,64]{1,0:T(8,128)} %bitcast.2, s32[8,8]{1,0:T(8,128)} %mid_source.1, s32[1]{0:T(128)S(6)} %copy.17.near_count, s32[8,128]{1,0:T(8,128)} %bitcast.3, bf16[8,4096]{1,0:T(8,128)(2,1)} %copy-done, bf16[8,4096]{1,0:T(8,128)(2,1)} %copy-done.1, ...), custom_call_target="tpu_custom_call" | custom-call | tf_op jit(solution)/shard_map/pallas_call | solution.py:436
  29.5 1.5 %copy.18 = bf16[8,4096]{1,0:T(8,128)(2,1)} copy(bf16[8,4096]{1,0:T(8,128)(2,1)} %shard_map.145) | data formatting | bytes 131072
Async XLA Ops:
  0.0 4.3 %collective-permute-start = (bf16[8,4096]{1,0:T(8,128)(2,1)}, bf16[8,4096]{1,0:T(8,128)(2,1)S(1)}, u32[]{:S(2)}, u32[]{:S(2)}) collective-permute-start(bf16[8,4096]{1,0:T(8,128)(2,1)} %charges_h.1), channel_id=1, source_target_pairs={{0,1},{1,2},{2,3},{3,4},{4,5},{5,6},{6,7},{7,8},{8,9},{9,10},{10,1... | collective-permute-start | bytes 196616 | tf_op jit(solution)/shard_map/ppermute | solution.py:429
  2.4 5.5 %collective-permute-start.1 = (bf16[8,4096]{1,0:T(8,128)(2,1)}, bf16[8,4096]{1,0:T(8,128)(2,1)S(1)}, u32[]{:S(2)}, u32[]{:S(2)}) collective-permute-start(bf16[8,4096]{1,0:T(8,128)(2,1)} %charges_h.1), channel_id=1, source_target_pairs={{1,0},{2,1},{3,2},{4,3},{5,4},{6,5},{7,6},{8,7},{9,8},{10,9},{11,1... | collective-permute-start | bytes 196616 | tf_op jit(solution)/shard_map/ppermute | solution.py:430
  4.4 3.5 %copy-start = (bf16[8,4096]{1,0:T(8,128)(2,1)}, bf16[8,4096]{1,0:T(8,128)(2,1)S(1)}, u32[]{:S(2)}) copy-start(bf16[8,4096]{1,0:T(8,128)(2,1)S(1)} %collective-permute-done.left_ref) | copy-start | bytes 196612
  7.8 0.6 %copy-start.1 = (bf16[8,4096]{1,0:T(8,128)(2,1)}, bf16[8,4096]{1,0:T(8,128)(2,1)S(1)}, u32[]{:S(2)}) copy-start(bf16[8,4096]{1,0:T(8,128)(2,1)S(1)} %collective-permute-done.1.right_ref) | copy-start | bytes 196612
